TPU v7x, 32 devices: a whole 2x2x4 slice. The times are simulated.
32 devices in a mesh: dp: 8 (over y, x, core), seq: 4 (over z).
Axes of the slice: x: 2, y: 2, z: 4, core: 2. Of those that a mesh axis runs over, the one named last changes fastest.
Arguments:
- tokens: bfloat16 [8, 2048, 1024], P('dp', 'seq'), may hold values from -45 to 45
- expand_value: bfloat16 [1024, 2816], P(None, 'dp'), may hold values from -0.1875 to 0.1875
- expand_scale: bfloat16 [8, 2816], P(None, 'dp'), may hold values from 0.5 to 2
- shrink_value: bfloat16 [2816, 1024], P(None, 'dp'), may hold values from -0.109375 to 0.109375
- shrink_scale: bfloat16 [22, 1024], P(None, 'dp'), may hold values from 0.5 to 2
- project_value: bfloat16 [1024, 3072], P(None, 'dp'), may hold values from -0.1875 to 0.1875
- project_scale: bfloat16 [8, 3072], P(None, 'dp'), may hold values from 0.5 to 12, as said below
- output_value: bfloat16 [1024, 1024], P(None, 'dp'), may hold values from -0.1875 to 0.1875
- output_scale: bfloat16 [8, 1024], P(None, 'dp'), may hold values from 0.5 to 2
- widen_value: bfloat16 [1024, 2048], P(None, 'dp'), may hold values from -0.1875 to 0.1875
- widen_scale: bfloat16 [8, 2048], P(None, 'dp'), may hold values from 0.5 to 2
- narrow_value: bfloat16 [1024, 1024], P(None, 'dp'), may hold values from -0.1875 to 0.1875
- narrow_scale: bfloat16 [8, 1024], P(None, 'dp'), may hold values from 0.5 to 2
- kernel_taps: float32 [31, 1024], replicated, may hold values from -1 to 1
- gain_feed: float32 [1024], replicated, may hold values from 0.25 to 1.75
- gain_attend: float32 [1024], replicated, may hold values from 0.25 to 1.75
- gain_conv: float32 [1024], replicated, may hold values from 0.25 to 1.75
- gain_final: float32 [1024], replicated, may hold values from 0.25 to 1.75
- batch_scale: float32 [1024], replicated, may hold values from 0.5 to 2
- batch_shift: float32 [1024], replicated, may hold values from -3 to 3
Outputs:
- block_out: bfloat16 [8, 2048, 1024], P('dp', 'seq')
Inputs may be any that keep to these rules, and one draw needn't show every extreme that they name: `project_scale`: block scales of the joined projection.
All inputs are finite; a program needn't handle non-finite values.
Results may differ from a plain program's by a relative error of at most 0.017.
The roundings to bfloat16 on the way count: a program that leaves them out, or rounds other values in their place, can miss the bound.
Values may be sent and summed in bfloat16 or wider, within the bound.
No kernel may reach another device: no remote copies, remote signals or barrier semaphores. Data moves between devices by JAX's collectives and lax.ppermute only.
A program may use at most 128 MiB of HBM per device.

v0:
```python
import functools
import math

import jax
import jax.numpy as jnp
from jax import lax
from jax.experimental import pallas as pl
from jax.experimental.pallas import tpu as pltpu
from jax.sharding import PartitionSpec as P

HEAD = 64
KERNEL = 31
LANES = 128
HALO = 16
NT = (((1,), (1,)), ((), ()))


def dequant(value_grid, scale_grid):
    stretched = jnp.repeat(scale_grid.astype(jnp.float32), 128, axis=0)
    return (value_grid.astype(jnp.float32) * stretched).astype(jnp.bfloat16)


def own_rows_of(value_grid, scale_grid):
    return jnp.transpose(dequant(value_grid, scale_grid))


def gathered(rows):
    return lax.all_gather(rows, "dp", axis=0, tiled=True)


def product(left, right):
    return lax.dot_general(left, right, NT, preferred_element_type=jnp.float32)


def layer_norm(values, gain_row):
    average = jnp.mean(values, axis=-1, keepdims=True)
    centred = values - average
    energy = jnp.mean(centred * centred, axis=-1, keepdims=True)
    return centred * lax.rsqrt(energy + 1e-05) * gain_row


def partners(size, bit):
    return [(i, i ^ bit) for i in range(size)]


def send(array, bit):
    return lax.ppermute(array, "dp", partners(lax.axis_size("dp"), bit))


def far_bits():
    return [1 << b for b in range(1, lax.axis_size("dp").bit_length() - 1)]


def stage(held, bit):
    return held + [(far ^ bit, number, send(a, bit)) for far, number, a in held]


def first_stages(parts):
    bits = far_bits()
    return [
        ([(0, number, part)], [(bit, number, send(part, bit)) for bit in bits])
        for number, part in enumerate(parts)
    ]


def later_stages(sets):
    bits = far_bits()
    result = []
    for own, first in sets:
        number = own[0][1]
        order = bits if number % 2 == 0 else bits[::-1]
        by_bit = dict(zip(bits, first))
        held = list(own)
        for bit in order:
            held += [by_bit[bit]] + [(far ^ bit, n, send(a, bit)) for far, n, a in held[1:]]
        result += held
    return result


def crossed(held):
    return stage(held, 1)


def refilled(sets, arrays):
    arrays = list(arrays)
    return [
        tuple([(far, n, arrays.pop(0)) for far, n, _ in group] for group in pair) for pair in sets
    ]


def barrier(*trees):
    return lax.optimization_barrier(trees)


def copies(pieces, refs, target, sems, share):
    own = lax.axis_index("dp")
    made = []
    for index, ((far, number), ref) in enumerate(zip(pieces, refs)):
        start = (own ^ far) * share + number * ref.shape[0]
        start = pl.multiple_of(start, 16)
        made.append(
            pltpu.make_async_copy(ref, target.at[pl.ds(start, ref.shape[0]), :], sems.at[index])
        )
    return made


def kernel_norm(values, gain_row):
    scale = 1.0 / values.shape[1]
    average = jnp.sum(values, axis=1, keepdims=True) * scale
    centred = values - average
    energy = jnp.sum(centred * centred, axis=1, keepdims=True) * scale
    return centred * lax.rsqrt(energy + 1e-05) * gain_row


def silu(v):
    half = 0.5 * v
    return half + half * jnp.tanh(half)


def feed_kernel(chunks, pieces, share, edge, *refs):
    refs = list(refs)
    tokens = [refs.pop(0) for _ in range(chunks)]
    gain_feed, gain_attend, expand = refs.pop(0), refs.pop(0), refs.pop(0)
    shrink_refs = [refs.pop(0) for _ in pieces]
    attend_in, fed, fed_edge, held, expand_all, shrink_all, feed_in, hidden, total = refs[:9]
    token_sems, expand_sems, shrink_sems = refs[9:]
    step = pl.program_id(0)
    units, width = expand_all.shape
    block = 256

    token_copies = [
        pltpu.make_async_copy(t, held.at[i], token_sems.at[i]) for i, t in enumerate(tokens)
    ]
    expand_copies = [
        pltpu.make_async_copy(
            expand.at[pl.ds(n * block, block), :],
            expand_all.at[pl.ds(n * block, block), :],
            expand_sems.at[n],
        )
        for n in range(units // block)
    ]
    shrink_copies = copies(pieces, shrink_refs, shrink_all, shrink_sems, share)

    @pl.when(step == 0)
    def _():
        for copy in token_copies[:1] + expand_copies + shrink_copies + token_copies[1:]:
            copy.start()

    for i in range(chunks):
        @pl.when(step == i)
        def _(i=i):
            token_copies[i].wait()

    feed_in[...] = kernel_norm(held[step].astype(jnp.float32), gain_feed[...]).astype(jnp.bfloat16)

    @pl.when(step == 0)
    def _():
        for copy in expand_copies:
            copy.wait()

    for n in range(units // block):
        piece = slice(n * block, (n + 1) * block)
        hidden[:, piece] = silu(product(feed_in[...], expand_all[piece, :])).astype(jnp.bfloat16)

    @pl.when(step == 0)
    def _():
        for copy in shrink_copies:
            copy.wait()

    for n in range(width // block):
        piece = slice(n * block, (n + 1) * block)
        total[:, piece] = held[step, :, piece].astype(jnp.float32) + 0.5 * product(
            hidden[...], shrink_all[piece, :]
        )
    attend_in[...] = kernel_norm(total[...], gain_attend[...]).astype(jnp.bfloat16)

    @pl.when(step == 0)
    def _():
        fed[...] = total[...]

    @pl.when(step == edge[0])
    def _():
        fed_edge[...] = total[edge[1] : edge[1] + HALO, :]


def feed(chunks, edge, gain_feed, gain_attend, expand_full, shrink_pieces):
    rows, width = chunks[0].shape
    units = expand_full.shape[0]
    count = len(chunks)
    anywhere = pl.BlockSpec(memory_space=pltpu.HBM)
    row = pl.BlockSpec((1, width), lambda i: (0, 0))
    share = width // lax.axis_size("dp")
    return pl.pallas_call(
        functools.partial(feed_kernel, count, [p[:2] for p in shrink_pieces], share, edge),
        grid=(count,),
        out_shape=[
            jax.ShapeDtypeStruct((count * rows, width), jnp.bfloat16),
            jax.ShapeDtypeStruct((rows, width), jnp.float32),
            jax.ShapeDtypeStruct((HALO, width), jnp.float32),
        ],
        in_specs=[anywhere] * count + [row, row, anywhere] + [anywhere] * len(shrink_pieces),
        out_specs=[
            pl.BlockSpec((rows, width), lambda i: (i, 0)),
            pl.BlockSpec((rows, width), lambda i: (0, 0)),
            pl.BlockSpec((HALO, width), lambda i: (0, 0)),
        ],
        scratch_shapes=[
            pltpu.VMEM((count, rows, width), jnp.bfloat16),
            pltpu.VMEM((units, width), jnp.bfloat16),
            pltpu.VMEM((width, units), jnp.bfloat16),
            pltpu.VMEM((rows, width), jnp.bfloat16),
            pltpu.VMEM((rows, units), jnp.bfloat16),
            pltpu.VMEM((rows, width), jnp.float32),
            pltpu.SemaphoreType.DMA((count,)),
            pltpu.SemaphoreType.DMA((units // 256,)),
            pltpu.SemaphoreType.DMA((len(shrink_pieces),)),
        ],
        compiler_params=pltpu.CompilerParams(vmem_limit_bytes=48 << 20),
        cost_estimate=pl.CostEstimate(
            flops=4 * count * rows * width * units,
            bytes_accessed=4 * units * width + 4 * count * rows * width,
            transcendentals=count * rows * units,
        ),
        name="feed",
    )(
        *chunks, gain_feed[None], gain_attend[None], expand_full, *[p[2] for p in shrink_pieces]
    )


def project_kernel(inputs, pieces, share, *refs):
    refs = list(refs)
    query_source = refs.pop(0)
    sources = [refs.pop(0) for _ in range(inputs)]
    weight_refs = [refs.pop(0) for _ in pieces]
    queries = refs.pop(0)
    pairs = [refs.pop(0) for _ in range(inputs)]
    weights, sems = refs
    step = pl.program_id(0)
    block = queries.shape[1]
    made = copies(pieces, weight_refs, weights, sems, share)

    @pl.when(step == 0)
    def _():
        for copy in made:
            copy.start()
        for copy in made:
            copy.wait()

    piece = weights[pl.ds(pl.multiple_of(step * block, block), block), :]
    parts = weights.shape[1] // block

    @pl.when(step < parts)
    def _():
        queries[...] = product(query_source[...], piece).astype(jnp.bfloat16)

    @pl.when(step >= parts)
    def _():
        for source, pair in zip(sources, pairs):
            for start in range(0, source.shape[0], 512):
                rows = slice(start, min(start + 512, source.shape[0]))
                pair[rows, :] = product(source[rows, :], piece).astype(jnp.bfloat16)


def projected(query_source, sources, pieces):
    rows, width = query_source.shape
    block = 256
    parts = width // block
    share = 3 * width // lax.axis_size("dp")
    length = sum(s.shape[0] for s in sources)
    anywhere = pl.BlockSpec(memory_space=pltpu.HBM)
    return pl.pallas_call(
        functools.partial(project_kernel, len(sources), [p[:2] for p in pieces], share),
        grid=(3 * parts,),
        out_shape=[jax.ShapeDtypeStruct((rows, width), jnp.bfloat16)]
        + [jax.ShapeDtypeStruct((s.shape[0], 2 * width), jnp.bfloat16) for s in sources],
        in_specs=[pl.BlockSpec(s.shape, lambda i: (0, 0)) for s in (query_source, *sources)]
        + [anywhere] * len(pieces),
        out_specs=[pl.BlockSpec((rows, block), lambda i: (0, jnp.minimum(i, parts - 1)))]
        + [
            pl.BlockSpec((s.shape[0], block), lambda i: (0, jnp.maximum(i - parts, 0)))
            for s in sources
        ],
        scratch_shapes=[
            pltpu.VMEM((3 * width, width), jnp.bfloat16),
            pltpu.SemaphoreType.DMA((len(pieces),)),
        ],
        compiler_params=pltpu.CompilerParams(vmem_limit_bytes=56 << 20),
        cost_estimate=pl.CostEstimate(
            flops=2 * width * width * (rows + 2 * length),
            bytes_accessed=2 * width * (3 * width + rows + 3 * length),
            transcendentals=0,
        ),
        name="project",
    )(query_source, *sources, *[p[2] for p in pieces])


def attention_kernel(count, tile, q_ref, *refs):
    keys, values, out_ref = refs[:count], refs[count : 2 * count], refs[2 * count]
    rows = q_ref.shape[0]
    heads = LANES // HEAD
    lane = lax.broadcasted_iota(jnp.int32, (tile, LANES), 1) // HEAD
    factor = HEAD ** (-0.5) * math.log2(math.e)
    tiles = [(start, head) for start in range(0, rows, tile) for head in range(heads)]

    def scores_of(start, head):
        picked = jnp.where(lane == head, q_ref[start : start + tile, :], jnp.bfloat16(0))
        return [
            lax.dot_general(picked, k[...], NT, preferred_element_type=jnp.float32) for k in keys
        ]

    def context_of(scores):
        top = functools.reduce(jnp.maximum, [jnp.max(s, axis=1, keepdims=True) for s in scores])
        raised = [jnp.exp2((s - top) * factor) for s in scores]
        totals = sum(jnp.sum(r, axis=1, keepdims=True) for r in raised)
        mixed = sum(
            jnp.dot(r.astype(jnp.bfloat16), v[...], preferred_element_type=jnp.float32)
            for r, v in zip(raised, values)
        )
        return mixed / totals

    pending = scores_of(*tiles[0])
    merged = None
    for index, (start, head) in enumerate(tiles):
        scores = pending
        if index + 1 < len(tiles):
            pending = scores_of(*tiles[index + 1])
        mixed = context_of(scores)
        merged = mixed if head == 0 else jnp.where(lane == head, mixed, merged)
        if head == heads - 1:
            out_ref[start : start + tile, :] = merged.astype(jnp.bfloat16)


def attention(queries, pairs):
    rows, width = queries.shape
    count = len(pairs)
    length = sum(p.shape[0] for p in pairs)
    steps = width // LANES
    spec = pl.BlockSpec((rows, LANES), lambda h: (0, h))
    return pl.pallas_call(
        functools.partial(attention_kernel, count, rows // 2),
        grid=(steps,),
        out_shape=jax.ShapeDtypeStruct((rows, width), jnp.bfloat16),
        in_specs=[spec]
        + [pl.BlockSpec((p.shape[0], LANES), lambda h: (0, h)) for p in pairs]
        + [pl.BlockSpec((p.shape[0], LANES), lambda h: (0, h + steps)) for p in pairs],
        out_specs=spec,
        compiler_params=pltpu.CompilerParams(vmem_limit_bytes=40 << 20),
        cost_estimate=pl.CostEstimate(
            flops=16 * rows * length * width,
            bytes_accessed=4 * (rows + length) * width,
            transcendentals=rows * length * width // HEAD,
        ),
        name="attention",
    )(queries, *pairs, *pairs)


def tail_kernel(
    context, fed_before, fed_own, fed_after, weights,
    gain_conv, gain_final, taps, scale, shift,
    out, w_output, w_widen, w_narrow, stream, conv_in, gated, shifted, activated, sems,
):
    rows, width = out.shape
    total = rows + 2 * HALO
    block = 256
    devices, share = w_output.shape[:2]
    made = [
        pltpu.make_async_copy(weights.at[:, pl.ds(start, ref.shape[1]), :], ref, sems.at[index])
        for index, (start, ref) in enumerate(
            ((0, w_output), (share, w_widen), (3 * share, w_narrow))
        )
    ]
    for copy in made:
        copy.start()

    def rows_of(ref, start):
        each = ref.shape[1]
        return ref[start // each : (start + block) // each].reshape(block, width)

    made[0].wait()
    for start in range(0, width, block):
        columns = slice(start, start + block)
        mixed = product(context[...], rows_of(w_output, start))
        stream[0:HALO, columns] = fed_before[:, columns] + mixed[0:HALO]
        stream[HALO : HALO + rows, columns] = fed_own[:, columns] + mixed[HALO : HALO + rows]
        stream[HALO + rows :, columns] = fed_after[:, columns] + mixed[HALO + rows :]
    conv_in[...] = kernel_norm(stream[...], gain_conv[...]).astype(jnp.bfloat16)

    made[1].wait()
    place = lax.broadcasted_iota(jnp.int32, (total, block), 0)
    here, last = lax.axis_index("seq"), lax.axis_size("seq") - 1
    low = jnp.where(here == 0, HALO, 0)
    high = jnp.where(here == last, HALO + rows, total)
    inside = jnp.logical_and(place >= low, place < high)
    for start in range(0, width, block):
        columns = slice(start, start + block)
        left = product(conv_in[...], rows_of(w_widen, start))
        right = product(conv_in[...], rows_of(w_widen, width + start))
        gate = (left * (0.5 + 0.5 * jnp.tanh(0.5 * right))).astype(jnp.bfloat16)
        gated[:, columns] = jnp.where(inside, gate.astype(jnp.float32), 0.0)

    lead = HALO - KERNEL // 2
    tile = min(128, rows)

    def conv(index, carry):
        columns = pl.ds(pl.multiple_of(index * LANES, LANES), LANES)
        for residue in range(1, 8):
            shifted[residue, 0 : total - 8, :] = gated[residue : residue + total - 8, columns]
        for start in range(0, rows, tile):
            filtered = jnp.zeros((tile, LANES), jnp.float32)
            for tap in range(KERNEL):
                offset = tap + lead
                base = start + offset // 8 * 8
                if offset % 8 == 0:
                    piece = gated[base : base + tile, columns]
                else:
                    piece = shifted[offset % 8, base : base + tile, :]
                filtered = filtered + taps[tap : tap + 1, columns] * piece
            moved = filtered * scale[:, columns] + shift[:, columns]
            activated[start : start + tile, columns] = silu(moved).astype(jnp.bfloat16)
        return carry

    lax.fori_loop(0, width // LANES, conv, 0)

    made[2].wait()
    for start in range(0, width, block):
        columns = slice(start, start + block)
        stream[HALO : HALO + rows, columns] += product(activated[...], rows_of(w_narrow, start))
    out[...] = kernel_norm(stream[HALO : HALO + rows, :], gain_final[...]).astype(jnp.bfloat16)


def tail_of(context, fed_before, fed_own, fed_after, weights, gain_conv, gain_final, taps, scale, shift):
    rows, width = fed_own.shape
    total = rows + 2 * HALO
    devices = weights.shape[0]
    share = width // devices
    whole = pl.BlockSpec(memory_space=pltpu.VMEM)
    return pl.pallas_call(
        tail_kernel,
        out_shape=jax.ShapeDtypeStruct((rows, width), jnp.bfloat16),
        in_specs=[whole] * 4 + [pl.BlockSpec(memory_space=pltpu.HBM)] + [whole] * 5,
        out_specs=whole,
        scratch_shapes=[
            pltpu.VMEM((devices, share, width), jnp.bfloat16),
            pltpu.VMEM((devices, 2 * share, width), jnp.bfloat16),
            pltpu.VMEM((devices, share, width), jnp.bfloat16),
            pltpu.VMEM((total, width), jnp.float32),
            pltpu.VMEM((total, width), jnp.bfloat16),
            pltpu.VMEM((total, width), jnp.float32),
            pltpu.VMEM((8, total, LANES), jnp.float32),
            pltpu.VMEM((rows, width), jnp.bfloat16),
            pltpu.SemaphoreType.DMA((3,)),
        ],
        compiler_params=pltpu.CompilerParams(vmem_limit_bytes=48 << 20),
        cost_estimate=pl.CostEstimate(
            flops=8 * total * width * width + 2 * KERNEL * rows * width,
            bytes_accessed=8 * width * width + 10 * rows * width,
            transcendentals=3 * rows * width,
        ),
        name="tail",
    )(
        context, fed_before, fed_own, fed_after, weights,
        gain_conv[None], gain_final[None], taps, scale[None], shift[None],
    )


def body(
    tokens,
    expand_value,
    expand_scale,
    shrink_value,
    shrink_scale,
    project_value,
    project_scale,
    output_value,
    output_scale,
    widen_value,
    widen_scale,
    narrow_value,
    narrow_scale,
    kernel_taps,
    gain_feed,
    gain_attend,
    gain_conv,
    gain_final,
    batch_scale,
    batch_shift,
):
    count = lax.axis_size("seq")
    rows = tokens.shape[1]
    ring = [(i, (i + 1) % count) for i in range(count)]
    chunks = [tokens[0]]

    def pass_on():
        chunks.append(lax.ppermute(chunks[-1], "seq", ring))

    expand_full = gathered(own_rows_of(expand_value, expand_scale))
    shrink_sets = first_stages(jnp.split(own_rows_of(shrink_value, shrink_scale), 2))
    project_parts = jnp.split(own_rows_of(project_value, project_scale), 2)
    tail_rows = jnp.concatenate(
        [
            own_rows_of(output_value, output_scale),
            own_rows_of(widen_value, widen_scale),
            own_rows_of(narrow_value, narrow_scale),
        ],
        axis=0,
    )
    tail_weights = lax.all_gather(tail_rows, "dp", axis=0)
    pass_on()

    arrays, project_parts, chunks[-1] = barrier(
        [a for own, first in shrink_sets for _, _, a in own + first], project_parts, chunks[-1]
    )
    shrink_sets = refilled(shrink_sets, arrays)
    shrink_held = later_stages(shrink_sets)
    project_sets = first_stages(project_parts)
    pass_on()

    shrink_arrays, arrays, chunks[-1] = barrier(
        [a for _, _, a in shrink_held],
        [a for own, first in project_sets for _, _, a in own + first],
        chunks[-1],
    )
    shrink_held = [(*t[:2], a) for t, a in zip(shrink_held, shrink_arrays)]
    project_sets = refilled(project_sets, arrays)
    shrink_pieces = crossed(shrink_held)
    project_pieces = crossed(later_stages(project_sets))
    while len(chunks) < count:
        pass_on()

    attend_near, after_feed, fed_before = feed(
        chunks[:-1], (1, rows - HALO), gain_feed, gain_attend, expand_full, shrink_pieces
    )
    attend_far, _, fed_after = feed(
        chunks[-1:], (0, 0), gain_feed, gain_attend, expand_full, shrink_pieces
    )
    query_source = jnp.concatenate(
        [attend_near[2 * rows - HALO : 2 * rows], attend_near[:rows], attend_far[:HALO]], axis=0
    )
    queries, *pairs = projected(query_source, [attend_near, attend_far], project_pieces)
    context = attention(queries, pairs)
    return tail_of(
        context, fed_before, after_feed, fed_after, tail_weights,
        gain_conv, gain_final, kernel_taps, batch_scale, batch_shift,
    )[None]


def solution(mesh):
    weights = (P(None, "dp"),) * 12
    return jax.shard_map(
        body,
        mesh=mesh,
        in_specs=(P("dp", "seq", None),) + weights + (P(),) * 7,
        out_specs=P("dp", "seq", None),
        check_vma=False,
    )
```

profile of v0, /device:TPU:0, one launch (start us, length us, event | category | flops | bytes accessed | tf_op | source)
XLA Modules:
  0.0 250.9 jit_solution(17033202020293908306)
XLA Ops:
  11.4 3.1 %collective-permute-start.4 = (bf16[512,1024]{1,0:T(8,128)(2,1)}, bf16[512,1024]{1,0:T(8,128)(2,1)}, u32[]{:S(2)}, u32[]{:S(2)}) collective-permute-start(bf16[512,1024]{1,0:T(8,128)(2,1)} %bitcast.refs_0_), channel_id=1, source_target_pairs={{0,1},{1,2},{2,3},{3,0},{4,5},{5,6},{6,7},{7,4},{8,9},{9,10},{10,1... | collective-permute-start | bytes 3145736 | tf_op jit(solution)/shard_map/ppermute | solution.py:494
  15.0 1.4 copy.27
  16.6 1.6 collective-permute-start
  18.2 1.5 collective-permute-start.1
  24.6 9.3 %collective-permute-done.refs_7_.refs_5_ = bf16[64,2816]{1,0:T(8,128)(2,1)S(1)} collective-permute-done((bf16[64,2816]{1,0:T(8,128)(2,1)S(1)}, bf16[64,2816]{1,0:T(8,128)(2,1)S(1)}, u32[]{:S(2)}, u32[]{:S(2)}) %collective-permute-start) | collective-permute-done | bytes 360480 | tf_op jit(solution)/shard_map/ppermute | solution.py:47
  33.9 2.4 collective-permute-done.1.refs_8_.refs_6_
  36.3 5.7 %collective-permute-done.2.refs_12_.refs_10_ = bf16[64,2816]{1,0:T(8,128)(2,1)S(1)} collective-permute-done((bf16[64,2816]{1,0:T(8,128)(2,1)S(1)}, bf16[64,2816]{1,0:T(8,128)(2,1)S(1)}, u32[]{:S(2)}, u32[]{:S(2)}) %collective-permute-start.2) | collective-permute-done | bytes 360480 | tf_op jit(solution)/shard_map/ppermute | solution.py:47
  43.2 1.6 collective-permute-start.11
  44.8 1.5 collective-permute-start.5
  46.9 1.5 collective-permute-start.7
  48.9 14.9 %collective-permute-done.5.refs_9_.refs_7_ = bf16[64,2816]{1,0:T(8,128)(2,1)S(1)} collective-permute-done((bf16[64,2816]{1,0:T(8,128)(2,1)S(1)}, bf16[64,2816]{1,0:T(8,128)(2,1)S(1)}, u32[]{:S(2)}, u32[]{:S(2)}) %collective-permute-start.5) | collective-permute-done | bytes 360480 | tf_op jit(solution)/shard_map/ppermute | solution.py:47
  65.8 13.0 %collective-permute-done.7.refs_4_ = bf16[192,1024]{1,0:T(8,128)(2,1)} collective-permute-done((bf16[192,1024]{1,0:T(8,128)(2,1)}, bf16[192,1024]{1,0:T(8,128)(2,1)}, u32[]{:S(2)}, u32[]{:S(2)}) %collective-permute-start.7) | collective-permute-done | bytes 393248 | tf_op jit(solution)/shard_map/ppermute | solution.py:47
  78.8 7.2 %collective-permute-done.9.refs_9_ = bf16[192,1024]{1,0:T(8,128)(2,1)S(1)} collective-permute-done((bf16[192,1024]{1,0:T(8,128)(2,1)S(1)}, bf16[192,1024]{1,0:T(8,128)(2,1)S(1)}, u32[]{:S(2)}, u32[]{:S(2)}) %collective-permute-start.9) | collective-permute-done | bytes 393248 | tf_op jit(solution)/shard_map/ppermute | solution.py:47
  93.8 1.6 collective-permute-start.20
  97.5 10.0 %collective-permute-done.21.refs_6_ = bf16[192,1024]{1,0:T(8,128)(2,1)} collective-permute-done((bf16[192,1024]{1,0:T(8,128)(2,1)}, bf16[192,1024]{1,0:T(8,128)(2,1)}, u32[]{:S(2)}, u32[]{:S(2)}) %collective-permute-start.21) | collective-permute-done | bytes 393248 | tf_op jit(solution)/shard_map/ppermute | solution.py:47
  114.4 29.2 %feed.2 = (bf16[1536,1024]{1,0:T(8,128)(2,1)}, f32[512,1024]{1,0:T(8,128)}, f32[16,1024]{1,0:T(8,128)S(1)}) custom-call(bf16[512,1024]{1,0:T(8,128)(2,1)} %bitcast.refs_0_, bf16[512,1024]{1,0:T(8,128)(2,1)} %collective-permute-done.4.refs_1_, bf16[512,1024]{1,0:T(8,128)(2,1)} %collective-permute-done.11.refs_2_, f32[1,1024]{1,0:T(1,128)S(1)} %bitcast.49, ...), custom_call_target="tpu_custom_call" | custom-call | flops 17716740096 | bytes 17825792 | tf_op jit(solution)/shard_map/feed/pallas_call | solution.py:193
  145.0 12.4 %feed.3 = (bf16[512,1024]{1,0:T(8,128)(2,1)}, f32[512,1024]{1,0:T(8,128)}, f32[16,1024]{1,0:T(8,128)S(1)}) custom-call(bf16[512,1024]{1,0:T(8,128)(2,1)} %collective-permute-done.20.refs_0_, f32[1,1024]{1,0:T(1,128)S(1)} %bitcast.50, f32[1,1024]{1,0:T(1,128)S(1)} %bitcast.52, bf16[2816,1024]{1,0:T(8,128)(2,1)} %all-gather.4.cloned.1.call-done.refs_5_.refs_3_, ...), custom_call_target="tpu_custom_call" | custom-call | flops 5905580032 | bytes 13631488 | tf_op jit(solution)/shard_map/feed/pallas_call | solution.py:193
  157.4 1.3 slice.10
  163.2 20.4 %project.1 = (bf16[544,1024]{1,0:T(8,128)(2,1)}, bf16[1536,2048]{1,0:T(8,128)(2,1)}, bf16[512,2048]{1,0:T(8,128)(2,1)}) custom-call(bf16[544,1024]{1,0:T(8,128)(2,1)} %pad_maximum_fusion.refs_0_, bf16[1536,1024]{1,0:T(8,128)(2,1)} %get-tuple-element.55.refs_1_, bf16[512,1024]{1,0:T(8,128)(2,1)} %get-tuple-element.56.refs_2_, ...), custom_call_target="tpu_custom_call" | custom-call | flops 9730785280 | bytes 19988480 | tf_op jit(solution)/shard_map/project/pallas_call | solution.py:271
  183.6 2.8 %copy-done.22 = bf16[1536,2048]{1,0:T(8,128)(2,1)S(1)} copy-done((bf16[1536,2048]{1,0:T(8,128)(2,1)S(1)}, bf16[1536,2048]{1,0:T(8,128)(2,1)}, u32[]{:S(2)}) %copy-start.22) | copy-done | bytes 6291480
  186.4 1.6 copy-done.23
  189.2 27.7 %attention.1.context = bf16[544,1024]{1,0:T(8,128)(2,1)S(1)} custom-call(bf16[544,1024]{1,0:T(8,128)(2,1)S(1)} %copy-done.24, bf16[1536,2048]{1,0:T(8,128)(2,1)S(1)} %copy-done.22, bf16[512,2048]{1,0:T(8,128)(2,1)S(1)} %copy-done.23, bf16[1536,2048]{1,0:T(8,128)(2,1)S(1)} %copy-done.22, bf16[512,2048]{1,0:T(8,128)(2,1)S(1)} %copy-done.23), custom_call_target="tpu_custom_call" | custom-call | flops 18253611008 | bytes 10616832 | tf_op jit(solution)/shard_map/attention/pallas_call | solution.py:339
  217.1 12.1 %copy.32 = bf16[4096,1024]{1,0:T(8,128)(2,1)} copy(bf16[4096,1024]{0,1:T(8,128)(2,1)} %all-gather.6.cloned.1.call-done) | data formatting | bytes 16777216 | tf_op jit(solution)/shard_map/all_gather | solution.py:507
  229.2 14.8 %tail.1 = bf16[512,1024]{1,0:T(8,128)(2,1)} custom-call(bf16[544,1024]{1,0:T(8,128)(2,1)S(1)} %attention.1.context, f32[16,1024]{1,0:T(8,128)S(1)} %get-tuple-element.66.fed_before, f32[512,1024]{1,0:T(8,128)S(1)} %copy-done.21, f32[16,1024]{1,0:T(8,128)S(1)} %get-tuple-element.68.fed_after, bf16[8,512,1024]{2,1,0:T(8,128)(2,1)} %bitcast.57, ...), custom_call_target="tpu_custom_call" | custom-call | flops 4595908608 | bytes 13631488 | tf_op jit(solution)/shard_map/tail/pallas_call | solution.py:437
  (164 shorter events, 38.5 us)
Async XLA Ops:
  6.5 100.9 %all-gather.4.cloned.1.call-start = ((), (), s32[]{:S(2)}) async-start(), calls=%async_computation | async-start | bytes 6488064 | tf_op jit(solution)/shard_map/all_gather | solution.py:28
  9.2 207.8 %all-gather.6.cloned.1.call-start = ((), (), s32[]{:S(2)}) async-start(), calls=%async_computation.1 | async-start | bytes 9437184 | tf_op jit(solution)/shard_map/all_gather | solution.py:507
  11.4 31.8 %collective-permute-start.4 = (bf16[512,1024]{1,0:T(8,128)(2,1)}, bf16[512,1024]{1,0:T(8,128)(2,1)}, u32[]{:S(2)}, u32[]{:S(2)}) collective-permute-start(bf16[512,1024]{1,0:T(8,128)(2,1)} %bitcast.refs_0_), channel_id=1, source_target_pairs={{0,1},{1,2},{2,3},{3,0},{4,5},{5,6},{6,7},{7,4},{8,9},{9,10},{10,1... | collective-permute-start | bytes 3145736 | tf_op jit(solution)/shard_map/ppermute | solution.py:494
  16.6 17.3 %collective-permute-start = (bf16[64,2816]{1,0:T(8,128)(2,1)S(1)}, bf16[64,2816]{1,0:T(8,128)(2,1)S(1)}, u32[]{:S(2)}, u32[]{:S(2)}) collective-permute-start(bf16[64,2816]{1,0:T(8,128)(2,1)S(1)} %get-tuple-element.47.refs_6_.refs_4_), channel_id=1, source_target_pairs={{0,8},{4,12},{8,0},{12,4},{16,24},{20,28},{24,16},{28,20},{1,9},{5... | collective-permute-start | bytes 1081352 | tf_op jit(solution)/shard_map/ppermute | solution.py:47
  18.2 18.1 %collective-permute-start.1 = (bf16[64,2816]{1,0:T(8,128)(2,1)S(1)}, bf16[64,2816]{1,0:T(8,128)(2,1)S(1)}, u32[]{:S(2)}, u32[]{:S(2)}) collective-permute-start(bf16[64,2816]{1,0:T(8,128)(2,1)S(1)} %get-tuple-element.47.refs_6_.refs_4_), channel_id=1, source_target_pairs={{0,16},{4,20},{8,24},{12,28},{16,0},{20,4},{24,8},{28,12},{1,17},{... | collective-permute-start | bytes 1081352 | tf_op jit(solution)/shard_map/ppermute | solution.py:47
  19.7 22.3 %collective-permute-start.2 = (bf16[64,2816]{1,0:T(8,128)(2,1)S(1)}, bf16[64,2816]{1,0:T(8,128)(2,1)S(1)}, u32[]{:S(2)}, u32[]{:S(2)}) collective-permute-start(bf16[64,2816]{1,0:T(8,128)(2,1)S(1)} %get-tuple-element.51.refs_10_.refs_8_), channel_id=1, source_target_pairs={{0,8},{4,12},{8,0},{12,4},{16,24},{20,28},{24,16},{28,20},{1,9},{5... | collective-permute-start | bytes 1081352 | tf_op jit(solution)/shard_map/ppermute | solution.py:47
  20.2 23.0 %collective-permute-start.3 = (bf16[64,2816]{1,0:T(8,128)(2,1)S(1)}, bf16[64,2816]{1,0:T(8,128)(2,1)S(1)}, u32[]{:S(2)}, u32[]{:S(2)}) collective-permute-start(bf16[64,2816]{1,0:T(8,128)(2,1)S(1)} %get-tuple-element.51.refs_10_.refs_8_), channel_id=1, source_target_pairs={{0,16},{4,20},{8,24},{12,28},{16,0},{20,4},{24,8},{28,12},{1,17},{... | collective-permute-start | bytes 1081352 | tf_op jit(solution)/shard_map/ppermute | solution.py:47
  43.2 42.8 %collective-permute-start.11 = (bf16[512,1024]{1,0:T(8,128)(2,1)}, bf16[512,1024]{1,0:T(8,128)(2,1)}, u32[]{:S(2)}, u32[]{:S(2)}) collective-permute-start(bf16[512,1024]{1,0:T(8,128)(2,1)} %collective-permute-done.4.refs_1_), channel_id=1, source_target_pairs={{0,1},{1,2},{2,3},{3,0},{4,5},{5,6},{6,7},{7,4},{8,9},{9,10},{10,1... | collective-permute-start | bytes 3145736 | tf_op jit(solution)/shard_map/ppermute | solution.py:494
  44.8 19.0 %collective-permute-start.5 = (bf16[64,2816]{1,0:T(8,128)(2,1)S(1)}, bf16[64,2816]{1,0:T(8,128)(2,1)S(1)}, u32[]{:S(2)}, u32[]{:S(2)}) collective-permute-start(bf16[64,2816]{1,0:T(8,128)(2,1)S(1)} %collective-permute-done.refs_7_.refs_5_), channel_id=1, source_target_pairs={{0,16},{4,20},{8,24},{12,28},{16,0},{20,4},{24,8},{28,12},{1,17},{... | collective-permute-start | bytes 1081352 | tf_op jit(solution)/shard_map/ppermute | solution.py:47
  46.3 19.0 %collective-permute-start.6 = (bf16[64,2816]{1,0:T(8,128)(2,1)S(1)}, bf16[64,2816]{1,0:T(8,128)(2,1)S(1)}, u32[]{:S(2)}, u32[]{:S(2)}) collective-permute-start(bf16[64,2816]{1,0:T(8,128)(2,1)S(1)} %collective-permute-done.3.refs_11_.refs_9_), channel_id=1, source_target_pairs={{0,8},{4,12},{8,0},{12,4},{16,24},{20,28},{24,16},{28,20},{1,9},{5... | collective-permute-start | bytes 1081352 | tf_op jit(solution)/shard_map/ppermute | solution.py:47
  46.9 32.0 %collective-permute-start.7 = (bf16[192,1024]{1,0:T(8,128)(2,1)}, bf16[192,1024]{1,0:T(8,128)(2,1)}, u32[]{:S(2)}, u32[]{:S(2)}) collective-permute-start(bf16[192,1024]{1,0:T(8,128)(2,1)} %get-tuple-element.57.refs_3_), channel_id=1, source_target_pairs={{0,8},{4,12},{8,0},{12,4},{16,24},{20,28},{24,16},{28,20},{1,9},{5... | collective-permute-start | bytes 1179656 | tf_op jit(solution)/shard_map/ppermute | solution.py:47
  48.4 30.5 %collective-permute-start.8 = (bf16[192,1024]{1,0:T(8,128)(2,1)}, bf16[192,1024]{1,0:T(8,128)(2,1)}, u32[]{:S(2)}, u32[]{:S(2)}) collective-permute-start(bf16[192,1024]{1,0:T(8,128)(2,1)} %get-tuple-element.57.refs_3_), channel_id=1, source_target_pairs={{0,16},{4,20},{8,24},{12,28},{16,0},{20,4},{24,8},{28,12},{1,17},{... | collective-permute-start | bytes 1179656 | tf_op jit(solution)/shard_map/ppermute | solution.py:47
  63.8 22.2 %collective-permute-start.9 = (bf16[192,1024]{1,0:T(8,128)(2,1)S(1)}, bf16[192,1024]{1,0:T(8,128)(2,1)S(1)}, u32[]{:S(2)}, u32[]{:S(2)}) collective-permute-start(bf16[192,1024]{1,0:T(8,128)(2,1)S(1)} %get-tuple-element.60.refs_7_), channel_id=1, source_target_pairs={{0,8},{4,12},{8,0},{12,4},{16,24},{20,28},{24,16},{28,20},{1,9},{5... | collective-permute-start | bytes 1179656 | tf_op jit(solution)/shard_map/ppermute | solution.py:47
  65.3 20.7 %collective-permute-start.10 = (bf16[192,1024]{1,0:T(8,128)(2,1)S(1)}, bf16[192,1024]{1,0:T(8,128)(2,1)}, u32[]{:S(2)}, u32[]{:S(2)}) collective-permute-start(bf16[192,1024]{1,0:T(8,128)(2,1)S(1)} %get-tuple-element.60.refs_7_), channel_id=1, source_target_pairs={{0,16},{4,20},{8,24},{12,28},{16,0},{20,4},{24,8},{28,12},{1,17},{... | collective-permute-start | bytes 1179656 | tf_op jit(solution)/shard_map/ppermute | solution.py:47
  87.8 19.6 %collective-permute-start.21 = (bf16[192,1024]{1,0:T(8,128)(2,1)}, bf16[192,1024]{1,0:T(8,128)(2,1)}, u32[]{:S(2)}, u32[]{:S(2)}) collective-permute-start(bf16[192,1024]{1,0:T(8,128)(2,1)} %collective-permute-done.7.refs_4_), channel_id=1, source_target_pairs={{0,16},{4,20},{8,24},{12,28},{16,0},{20,4},{24,8},{28,12},{1,17},{... | collective-permute-start | bytes 1179656 | tf_op jit(solution)/shard_map/ppermute | solution.py:47
  93.1 51.1 %collective-permute-start.24 = (bf16[192,1024]{1,0:T(8,128)(2,1)}, bf16[192,1024]{1,0:T(8,128)(2,1)}, u32[]{:S(2)}, u32[]{:S(2)}) collective-permute-start(bf16[192,1024]{1,0:T(8,128)(2,1)} %collective-permute-done.7.refs_4_), channel_id=1, source_target_pairs={{0,4},{4,0},{8,12},{12,8},{16,20},{20,16},{24,28},{28,24},{1,5},{5... | collective-permute-start | bytes 1179656 | tf_op jit(solution)/shard_map/ppermute | solution.py:47
  93.8 50.9 %collective-permute-start.20 = (bf16[512,1024]{1,0:T(8,128)(2,1)}, bf16[512,1024]{1,0:T(8,128)(2,1)}, u32[]{:S(2)}, u32[]{:S(2)}) collective-permute-start(bf16[512,1024]{1,0:T(8,128)(2,1)} %collective-permute-done.11.refs_2_), channel_id=1, source_target_pairs={{0,1},{1,2},{2,3},{3,0},{4,5},{5,6},{6,7},{7,4},{8,9},{9,10},{10,1... | collective-permute-start | bytes 3145736 | tf_op jit(solution)/shard_map/ppermute | solution.py:494
  96.2 47.4 %collective-permute-start.22 = (bf16[192,1024]{1,0:T(8,128)(2,1)}, bf16[192,1024]{1,0:T(8,128)(2,1)}, u32[]{:S(2)}, u32[]{:S(2)}) collective-permute-start(bf16[192,1024]{1,0:T(8,128)(2,1)} %collective-permute-done.10.refs_8_), channel_id=1, source_target_pairs={{0,8},{4,12},{8,0},{12,4},{16,24},{20,28},{24,16},{28,20},{1,9},{5... | collective-permute-start | bytes 1179656 | tf_op jit(solution)/shard_map/ppermute | solution.py:47
  97.5 46.5 %collective-permute-start.23 = (bf16[192,1024]{1,0:T(8,128)(2,1)}, bf16[192,1024]{1,0:T(8,128)(2,1)}, u32[]{:S(2)}, u32[]{:S(2)}) collective-permute-start(bf16[192,1024]{1,0:T(8,128)(2,1)} %get-tuple-element.57.refs_3_), channel_id=1, source_target_pairs={{0,4},{4,0},{8,12},{12,8},{16,20},{20,16},{24,28},{28,24},{1,5},{5... | collective-permute-start | bytes 1179656 | tf_op jit(solution)/shard_map/ppermute | solution.py:47
  107.4 37.1 %collective-permute-start.25 = (bf16[192,1024]{1,0:T(8,128)(2,1)}, bf16[192,1024]{1,0:T(8,128)(2,1)}, u32[]{:S(2)}, u32[]{:S(2)}) collective-permute-start(bf16[192,1024]{1,0:T(8,128)(2,1)} %collective-permute-done.8.refs_5_), channel_id=1, source_target_pairs={{0,4},{4,0},{8,12},{12,8},{16,20},{20,16},{24,28},{28,24},{1,5},{5... | collective-permute-start | bytes 1179656 | tf_op jit(solution)/shard_map/ppermute | solution.py:47
  143.6 17.7 %collective-permute-start.28 = (bf16[192,1024]{1,0:T(8,128)(2,1)}, bf16[192,1024]{1,0:T(8,128)(2,1)S(1)}, u32[]{:S(2)}, u32[]{:S(2)}) collective-permute-start(bf16[192,1024]{1,0:T(8,128)(2,1)} %collective-permute-done.10.refs_8_), channel_id=1, source_target_pairs={{0,4},{4,0},{8,12},{12,8},{16,20},{20,16},{24,28},{28,24},{1,5},{5... | collective-permute-start | bytes 1179656 | tf_op jit(solution)/shard_map/ppermute | solution.py:47
  144.0 17.3 %collective-permute-start.27 = (bf16[192,1024]{1,0:T(8,128)(2,1)S(1)}, bf16[192,1024]{1,0:T(8,128)(2,1)S(1)}, u32[]{:S(2)}, u32[]{:S(2)}) collective-permute-start(bf16[192,1024]{1,0:T(8,128)(2,1)S(1)} %copy-done.30), channel_id=1, source_target_pairs={{0,4},{4,0},{8,12},{12,8},{16,20},{20,16},{24,28},{28,24},{1,5},{5... | collective-permute-start | bytes 1179656 | tf_op jit(solution)/shard_map/ppermute | solution.py:47
  144.2 17.1 %collective-permute-start.29 = (bf16[192,1024]{1,0:T(8,128)(2,1)S(1)}, bf16[192,1024]{1,0:T(8,128)(2,1)S(1)}, u32[]{:S(2)}, u32[]{:S(2)}) collective-permute-start(bf16[192,1024]{1,0:T(8,128)(2,1)S(1)} %copy-done.39), channel_id=1, source_target_pairs={{0,4},{4,0},{8,12},{12,8},{16,20},{20,16},{24,28},{28,24},{1,5},{5... | collective-permute-start | bytes 1179656 | tf_op jit(solution)/shard_map/ppermute | solution.py:47
  144.5 16.8 %collective-permute-start.26 = (bf16[192,1024]{1,0:T(8,128)(2,1)}, bf16[192,1024]{1,0:T(8,128)(2,1)S(1)}, u32[]{:S(2)}, u32[]{:S(2)}) collective-permute-start(bf16[192,1024]{1,0:T(8,128)(2,1)} %collective-permute-done.21.refs_6_), channel_id=1, source_target_pairs={{0,4},{4,0},{8,12},{12,8},{16,20},{20,16},{24,28},{28,24},{1,5},{5... | collective-permute-start | bytes 1179656 | tf_op jit(solution)/shard_map/ppermute | solution.py:47
  (54 other events, 462.8 us)
Sparse Core Ops, SparseCore 0:
  9.4 68.4 all-gather.3
  79.8 63.1 all-gather.5
where the time goes:
time: 252 us; the launch traced here: 251 us
  Pallas kernels  105 us (42%)
  waiting for transfers between devices  65 us (26%)
  local copies, waits for them, and re-layouts  42.5 us (17%)
  starting transfers between devices  20.6 us (8%)
  between operations  13.9 us (6%)
  other arithmetic  4.36 us (2%)
    ppermute x28, waiting for transfers between devices, send(): return lax.ppermute(array, 'dp', partners(lax.axis_size('dp'), bit))  65 us
    pallas_call x2, Pallas kernels, feed(): pl.pallas_call(functools.partial(feed_kernel, count, [p[:2] for p in shri...  41.6 us
    pallas_call x1, Pallas kernels, attention(): pl.pallas_call(functools.partial(attention_kernel, count, rows // 2), gri...  27.7 us
    unnamed x92, local copies, waits for them, and re-layouts  24.2 us
    pallas_call x1, Pallas kernels, projected(): pl.pallas_call(functools.partial(project_kernel, len(sources), [p[:2] for...  20.4 us
    pallas_call x1, Pallas kernels, tail_of(): pl.pallas_call(tail_kernel, out_shape=jax.ShapeDtypeStruct((rows, width),...  14.8 us
    ppermute x28, starting transfers between devices, send(): return lax.ppermute(array, 'dp', partners(lax.axis_size('dp'), bit))  14.3 us
    all_gather x1, local copies, waits for them, and re-layouts, body(): tail_weights = lax.all_gather(tail_rows, 'dp', axis=0)  12.1 us
  transfers between devices with their start and end apart: 33, of which 9 were waited for; matrix products, arithmetic and copies ran while one was open for 4% of the time, Pallas kernels for 36%

commit v1 on v0

--- a/solution.py
+++ b/solution.py
@@ -5,6 +5,7 @@
 import jax.numpy as jnp
 from jax import lax
 from jax.experimental import pallas as pl
+from jax.experimental.layout import Layout, with_layout_constraint
 from jax.experimental.pallas import tpu as pltpu
 from jax.sharding import PartitionSpec as P
 
@@ -12,6 +13,7 @@
 KERNEL = 31
 LANES = 128
 HALO = 16
+VMEM = 60 << 20
 NT = (((1,), (1,)), ((), ()))
 
 
@@ -92,16 +94,32 @@
     return lax.optimization_barrier(trees)
 
 
+def half_of(share):
+    return -(-share // 32) * 16
+
+
+def halved(rows):
+    return [rows[: half_of(rows.shape[0])], rows[half_of(rows.shape[0]) :]]
+
+
 def copies(pieces, refs, target, sems, share):
     own = lax.axis_index("dp")
     made = []
-    for index, ((far, number), ref) in enumerate(zip(pieces, refs)):
-        start = (own ^ far) * share + number * ref.shape[0]
-        start = pl.multiple_of(start, 16)
-        made.append(
-            pltpu.make_async_copy(ref, target.at[pl.ds(start, ref.shape[0]), :], sems.at[index])
-        )
+    for (far, number), ref in zip(pieces, refs):
+        owner = own ^ far
+        start = pl.multiple_of(owner * share + number * half_of(share), 16)
+        rows = target.at[pl.ds(start, ref.shape[0]), :]
+        made.append(pltpu.make_async_copy(ref, rows, sems.at[owner, number]))
     return made
+
+
+def wait_rows(target, sems, share, owners):
+    half = half_of(share)
+    for owner in owners:
+        for number in range(2):
+            start = owner * share + number * half
+            rows = target.at[start : start + (share - half if number else half), :]
+            pltpu.make_async_copy(rows, rows, sems.at[owner, number]).wait()
 
 
 def kernel_norm(values, gain_row):
@@ -117,13 +135,15 @@
     return half + half * jnp.tanh(half)
 
 
-def feed_kernel(chunks, pieces, share, edge, *refs):
+def feed_kernel(chunks, pieces, share, edge, keep, *refs):
     refs = list(refs)
     tokens = [refs.pop(0) for _ in range(chunks)]
     gain_feed, gain_attend, expand = refs.pop(0), refs.pop(0), refs.pop(0)
     shrink_refs = [refs.pop(0) for _ in pieces]
-    attend_in, fed, fed_edge, held, expand_all, shrink_all, feed_in, hidden, total = refs[:9]
-    token_sems, expand_sems, shrink_sems = refs[9:]
+    attend_in, fed_edge = refs.pop(0), refs.pop(0)
+    fed = refs.pop(0) if keep else None
+    held, expand_all, shrink_all, feed_in, hidden, total = refs[:6]
+    token_sems, expand_sems, shrink_sems = refs[6:]
     step = pl.program_id(0)
     units, width = expand_all.shape
     block = 256
@@ -164,8 +184,7 @@
 
     @pl.when(step == 0)
     def _():
-        for copy in shrink_copies:
-            copy.wait()
+        wait_rows(shrink_all, shrink_sems, share, range(width // share))
 
     for n in range(width // block):
         piece = slice(n * block, (n + 1) * block)
@@ -174,16 +193,18 @@
         )
     attend_in[...] = kernel_norm(total[...], gain_attend[...]).astype(jnp.bfloat16)
 
-    @pl.when(step == 0)
-    def _():
-        fed[...] = total[...]
+    if fed is not None:
+
+        @pl.when(step == 0)
+        def _():
+            fed[...] = total[...]
 
     @pl.when(step == edge[0])
     def _():
         fed_edge[...] = total[edge[1] : edge[1] + HALO, :]
 
 
-def feed(chunks, edge, gain_feed, gain_attend, expand_full, shrink_pieces):
+def feed(chunks, edge, keep, gain_feed, gain_attend, expand_full, shrink_pieces):
     rows, width = chunks[0].shape
     units = expand_full.shape[0]
     count = len(chunks)
@@ -191,19 +212,19 @@
     row = pl.BlockSpec((1, width), lambda i: (0, 0))
     share = width // lax.axis_size("dp")
     return pl.pallas_call(
-        functools.partial(feed_kernel, count, [p[:2] for p in shrink_pieces], share, edge),
+        functools.partial(feed_kernel, count, [p[:2] for p in shrink_pieces], share, edge, keep),
         grid=(count,),
         out_shape=[
             jax.ShapeDtypeStruct((count * rows, width), jnp.bfloat16),
-            jax.ShapeDtypeStruct((rows, width), jnp.float32),
             jax.ShapeDtypeStruct((HALO, width), jnp.float32),
-        ],
+        ]
+        + [jax.ShapeDtypeStruct((rows, width), jnp.float32)] * keep,
         in_specs=[anywhere] * count + [row, row, anywhere] + [anywhere] * len(shrink_pieces),
         out_specs=[
             pl.BlockSpec((rows, width), lambda i: (i, 0)),
-            pl.BlockSpec((rows, width), lambda i: (0, 0)),
             pl.BlockSpec((HALO, width), lambda i: (0, 0)),
-        ],
+        ]
+        + [pl.BlockSpec((rows, width), lambda i: (0, 0))] * keep,
         scratch_shapes=[
             pltpu.VMEM((count, rows, width), jnp.bfloat16),
             pltpu.VMEM((units, width), jnp.bfloat16),
@@ -213,9 +234,9 @@
             pltpu.VMEM((rows, width), jnp.float32),
             pltpu.SemaphoreType.DMA((count,)),
             pltpu.SemaphoreType.DMA((units // 256,)),
-            pltpu.SemaphoreType.DMA((len(shrink_pieces),)),
+            pltpu.SemaphoreType.DMA((len(shrink_pieces) // 2, 2)),
         ],
-        compiler_params=pltpu.CompilerParams(vmem_limit_bytes=48 << 20),
+        compiler_params=pltpu.CompilerParams(vmem_limit_bytes=VMEM),
         cost_estimate=pl.CostEstimate(
             flops=4 * count * rows * width * units,
             bytes_accessed=4 * units * width + 4 * count * rows * width,
@@ -227,131 +248,141 @@
     )
 
 
-def project_kernel(inputs, pieces, share, *refs):
-    refs = list(refs)
-    query_source = refs.pop(0)
-    sources = [refs.pop(0) for _ in range(inputs)]
-    weight_refs = [refs.pop(0) for _ in pieces]
-    queries = refs.pop(0)
-    pairs = [refs.pop(0) for _ in range(inputs)]
-    weights, sems = refs
-    step = pl.program_id(0)
-    block = queries.shape[1]
+def attend_kernel(pieces, share, *refs):
+    near, far = refs[:2]
+    weight_refs = refs[2 : 2 + len(pieces)]
+    out_ref, inputs, query_rows, weights, queries, keys, values, sems, row_sems = refs[
+        2 + len(pieces) :
+    ]
+    step, steps = pl.program_id(0), pl.num_programs(0)
+    length, width = inputs.shape
+    rows = query_rows.shape[0] - 2 * HALO
+    pairs = width // LANES
     made = copies(pieces, weight_refs, weights, sems, share)
+    row_copies = [
+        pltpu.make_async_copy(source, target, row_sems.at[index])
+        for index, (source, target) in enumerate(
+            (
+                (near.at[0:rows, :], query_rows.at[HALO : HALO + rows, :]),
+                (near.at[2 * rows - HALO : 2 * rows, :], query_rows.at[0:HALO, :]),
+                (far.at[0:HALO, :], query_rows.at[HALO + rows :, :]),
+                (near, inputs.at[0 : length - rows, :]),
+                (far, inputs.at[length - rows :, :]),
+            )
+        )
+    ]
+    soon = sorted({(part * width + pair * LANES) // share for part in range(3) for pair in (0, 1)})
+
+    def project_queries(pair, slot):
+        picked = weights[pl.ds(pl.multiple_of(pair * LANES, LANES), LANES), :]
+        queries[slot] = product(query_rows[...], picked).astype(jnp.bfloat16)
+
+    def project_pair(pair, slot, start, stop):
+        first = pl.ds(pl.multiple_of(width + pair * LANES, LANES), LANES)
+        second = pl.ds(pl.multiple_of(2 * width + pair * LANES, LANES), LANES)
+        both = jnp.concatenate([weights[first, :], weights[second, :]], axis=0)
+        made_rows = product(inputs[start:stop, :], both).astype(jnp.bfloat16)
+        keys[slot, start:stop, :] = made_rows[:, :LANES]
+        values[slot, start:stop, :] = made_rows[:, LANES:]
 
     @pl.when(step == 0)
     def _():
-        for copy in made:
+        for copy in row_copies + made:
             copy.start()
-        for copy in made:
+        for copy in row_copies:
             copy.wait()
-
-    piece = weights[pl.ds(pl.multiple_of(step * block, block), block), :]
-    parts = weights.shape[1] // block
-
-    @pl.when(step < parts)
-    def _():
-        queries[...] = product(query_source[...], piece).astype(jnp.bfloat16)
-
-    @pl.when(step >= parts)
-    def _():
-        for source, pair in zip(sources, pairs):
-            for start in range(0, source.shape[0], 512):
-                rows = slice(start, min(start + 512, source.shape[0]))
-                pair[rows, :] = product(source[rows, :], piece).astype(jnp.bfloat16)
-
-
-def projected(query_source, sources, pieces):
-    rows, width = query_source.shape
-    block = 256
-    parts = width // block
-    share = 3 * width // lax.axis_size("dp")
-    length = sum(s.shape[0] for s in sources)
-    anywhere = pl.BlockSpec(memory_space=pltpu.HBM)
-    return pl.pallas_call(
-        functools.partial(project_kernel, len(sources), [p[:2] for p in pieces], share),
-        grid=(3 * parts,),
-        out_shape=[jax.ShapeDtypeStruct((rows, width), jnp.bfloat16)]
-        + [jax.ShapeDtypeStruct((s.shape[0], 2 * width), jnp.bfloat16) for s in sources],
-        in_specs=[pl.BlockSpec(s.shape, lambda i: (0, 0)) for s in (query_source, *sources)]
-        + [anywhere] * len(pieces),
-        out_specs=[pl.BlockSpec((rows, block), lambda i: (0, jnp.minimum(i, parts - 1)))]
-        + [
-            pl.BlockSpec((s.shape[0], block), lambda i: (0, jnp.maximum(i - parts, 0)))
-            for s in sources
-        ],
-        scratch_shapes=[
-            pltpu.VMEM((3 * width, width), jnp.bfloat16),
-            pltpu.SemaphoreType.DMA((len(pieces),)),
-        ],
-        compiler_params=pltpu.CompilerParams(vmem_limit_bytes=56 << 20),
-        cost_estimate=pl.CostEstimate(
-            flops=2 * width * width * (rows + 2 * length),
-            bytes_accessed=2 * width * (3 * width + rows + 3 * length),
-            transcendentals=0,
-        ),
-        name="project",
-    )(query_source, *sources, *[p[2] for p in pieces])
-
-
-def attention_kernel(count, tile, q_ref, *refs):
-    keys, values, out_ref = refs[:count], refs[count : 2 * count], refs[2 * count]
-    rows = q_ref.shape[0]
+        wait_rows(weights, sems, share, soon)
+        project_queries(0, 0)
+        for start in range(0, length, rows):
+            project_pair(0, 0, start, start + rows)
+
+    @pl.when(step == 1)
+    def _():
+        rest = [owner for owner in range(3 * width // share) if owner not in soon]
+        wait_rows(weights, sems, share, rest)
+
+    slot = lax.rem(step, 2)
     heads = LANES // HEAD
+    tile = query_rows.shape[0] // 2
     lane = lax.broadcasted_iota(jnp.int32, (tile, LANES), 1) // HEAD
     factor = HEAD ** (-0.5) * math.log2(math.e)
-    tiles = [(start, head) for start in range(0, rows, tile) for head in range(heads)]
+    tiles = [(start, head) for start in (0, tile) for head in range(heads)]
+    blocks = [slice(start, start + rows) for start in range(0, length, rows)]
 
     def scores_of(start, head):
-        picked = jnp.where(lane == head, q_ref[start : start + tile, :], jnp.bfloat16(0))
-        return [
-            lax.dot_general(picked, k[...], NT, preferred_element_type=jnp.float32) for k in keys
-        ]
+        picked = jnp.where(lane == head, queries[slot, start : start + tile, :], jnp.bfloat16(0))
+        return [product(picked, keys[slot, block, :]) for block in blocks]
 
     def context_of(scores):
         top = functools.reduce(jnp.maximum, [jnp.max(s, axis=1, keepdims=True) for s in scores])
         raised = [jnp.exp2((s - top) * factor) for s in scores]
         totals = sum(jnp.sum(r, axis=1, keepdims=True) for r in raised)
         mixed = sum(
-            jnp.dot(r.astype(jnp.bfloat16), v[...], preferred_element_type=jnp.float32)
-            for r, v in zip(raised, values)
+            jnp.dot(
+                r.astype(jnp.bfloat16),
+                values[slot, block, :],
+                preferred_element_type=jnp.float32,
+            )
+            for r, block in zip(raised, blocks)
         )
         return mixed / totals
 
-    pending = scores_of(*tiles[0])
-    merged = None
-    for index, (start, head) in enumerate(tiles):
-        scores = pending
-        if index + 1 < len(tiles):
-            pending = scores_of(*tiles[index + 1])
-        mixed = context_of(scores)
-        merged = mixed if head == 0 else jnp.where(lane == head, mixed, merged)
-        if head == heads - 1:
-            out_ref[start : start + tile, :] = merged.astype(jnp.bfloat16)
-
-
-def attention(queries, pairs):
-    rows, width = queries.shape
-    count = len(pairs)
-    length = sum(p.shape[0] for p in pairs)
-    steps = width // LANES
-    spec = pl.BlockSpec((rows, LANES), lambda h: (0, h))
+    def attend(project):
+        pending = scores_of(*tiles[0])
+        merged = None
+        for index, (start, head) in enumerate(tiles):
+            scores = pending
+            if index + 1 < len(tiles):
+                pending = scores_of(*tiles[index + 1])
+            if project:
+                if index == 0:
+                    project_queries(step + 1, 1 - slot)
+                for block in blocks[index :: len(tiles)]:
+                    project_pair(step + 1, 1 - slot, block.start, block.stop)
+            mixed = context_of(scores)
+            merged = mixed if head == 0 else jnp.where(lane == head, mixed, merged)
+            if head == heads - 1:
+                out_ref[start : start + tile, :] = merged.astype(jnp.bfloat16)
+
+    @pl.when(step < steps - 1)
+    def _():
+        attend(True)
+
+    @pl.when(step == steps - 1)
+    def _():
+        attend(False)
+
+
+def attention(near, far, pieces):
+    rows, width = far.shape
+    total = rows + 2 * HALO
+    length = near.shape[0] + rows
+    share = 3 * width // lax.axis_size("dp")
+    anywhere = pl.BlockSpec(memory_space=pltpu.HBM)
     return pl.pallas_call(
-        functools.partial(attention_kernel, count, rows // 2),
-        grid=(steps,),
-        out_shape=jax.ShapeDtypeStruct((rows, width), jnp.bfloat16),
-        in_specs=[spec]
-        + [pl.BlockSpec((p.shape[0], LANES), lambda h: (0, h)) for p in pairs]
-        + [pl.BlockSpec((p.shape[0], LANES), lambda h: (0, h + steps)) for p in pairs],
-        out_specs=spec,
-        compiler_params=pltpu.CompilerParams(vmem_limit_bytes=40 << 20),
+        functools.partial(attend_kernel, [p[:2] for p in pieces], share),
+        grid=(width // LANES,),
+        out_shape=jax.ShapeDtypeStruct((total, width), jnp.bfloat16),
+        in_specs=[anywhere] * (2 + len(pieces)),
+        out_specs=pl.BlockSpec((total, LANES), lambda h: (0, h)),
+        scratch_shapes=[
+            pltpu.VMEM((length, width), jnp.bfloat16),
+            pltpu.VMEM((total, width), jnp.bfloat16),
+            pltpu.VMEM((3 * width, width), jnp.bfloat16),
+            pltpu.VMEM((2, total, LANES), jnp.bfloat16),
+            pltpu.VMEM((2, length, LANES), jnp.bfloat16),
+            pltpu.VMEM((2, length, LANES), jnp.bfloat16),
+            pltpu.SemaphoreType.DMA((len(pieces) // 2, 2)),
+            pltpu.SemaphoreType.DMA((5,)),
+        ],
+        compiler_params=pltpu.CompilerParams(vmem_limit_bytes=VMEM),
         cost_estimate=pl.CostEstimate(
-            flops=16 * rows * length * width,
-            bytes_accessed=4 * (rows + length) * width,
-            transcendentals=rows * length * width // HEAD,
+            flops=16 * total * length * width + 2 * width * width * (total + 2 * length),
+            bytes_accessed=2 * width * (3 * width + 3 * total + length),
+            transcendentals=total * length * width // HEAD,
         ),
         name="attention",
-    )(queries, *pairs, *pairs)
+    )(near, far, *[p[2] for p in pieces])
 
 
 def tail_kernel(
@@ -450,7 +481,7 @@
             pltpu.VMEM((rows, width), jnp.bfloat16),
             pltpu.SemaphoreType.DMA((3,)),
         ],
-        compiler_params=pltpu.CompilerParams(vmem_limit_bytes=48 << 20),
+        compiler_params=pltpu.CompilerParams(vmem_limit_bytes=VMEM),
         cost_estimate=pl.CostEstimate(
             flops=8 * total * width * width + 2 * KERNEL * rows * width,
             bytes_accessed=8 * width * width + 10 * rows * width,
@@ -494,8 +525,8 @@
         chunks.append(lax.ppermute(chunks[-1], "seq", ring))
 
     expand_full = gathered(own_rows_of(expand_value, expand_scale))
-    shrink_sets = first_stages(jnp.split(own_rows_of(shrink_value, shrink_scale), 2))
-    project_parts = jnp.split(own_rows_of(project_value, project_scale), 2)
+    shrink_sets = first_stages(halved(own_rows_of(shrink_value, shrink_scale)))
+    project_parts = halved(own_rows_of(project_value, project_scale))
     tail_rows = jnp.concatenate(
         [
             own_rows_of(output_value, output_scale),
@@ -504,40 +535,39 @@
         ],
         axis=0,
     )
-    tail_weights = lax.all_gather(tail_rows, "dp", axis=0)
+    tail_rows = with_layout_constraint(tail_rows, Layout((0, 1)))
+    tail_weights = with_layout_constraint(
+        lax.all_gather(tail_rows, "dp", axis=0), Layout((0, 1, 2))
+    )
     pass_on()
 
-    arrays, project_parts, chunks[-1] = barrier(
-        [a for own, first in shrink_sets for _, _, a in own + first], project_parts, chunks[-1]
-    )
+    arrays, chunks[-1] = barrier([a for own, first in shrink_sets for _, _, a in own + first], chunks[-1])
     shrink_sets = refilled(shrink_sets, arrays)
     shrink_held = later_stages(shrink_sets)
+    pass_on()
+
+    arrays, project_parts, chunks[-1] = barrier(
+        [a for _, _, a in shrink_held], project_parts, chunks[-1]
+    )
+    shrink_held = [(*t[:2], a) for t, a in zip(shrink_held, arrays)]
+    shrink_pieces = crossed(shrink_held)
     project_sets = first_stages(project_parts)
-    pass_on()
-
-    shrink_arrays, arrays, chunks[-1] = barrier(
-        [a for _, _, a in shrink_held],
-        [a for own, first in project_sets for _, _, a in own + first],
-        chunks[-1],
-    )
-    shrink_held = [(*t[:2], a) for t, a in zip(shrink_held, shrink_arrays)]
-    project_sets = refilled(project_sets, arrays)
-    shrink_pieces = crossed(shrink_held)
-    project_pieces = crossed(later_stages(project_sets))
     while len(chunks) < count:
         pass_on()
 
-    attend_near, after_feed, fed_before = feed(
-        chunks[:-1], (1, rows - HALO), gain_feed, gain_attend, expand_full, shrink_pieces
-    )
-    attend_far, _, fed_after = feed(
-        chunks[-1:], (0, 0), gain_feed, gain_attend, expand_full, shrink_pieces
-    )
-    query_source = jnp.concatenate(
-        [attend_near[2 * rows - HALO : 2 * rows], attend_near[:rows], attend_far[:HALO]], axis=0
-    )
-    queries, *pairs = projected(query_source, [attend_near, attend_far], project_pieces)
-    context = attention(queries, pairs)
+    attend_near, fed_before, after_feed = feed(
+        chunks[:-1], (1, rows - HALO), True, gain_feed, gain_attend, expand_full, shrink_pieces
+    )
+    attend_near, arrays = barrier(
+        attend_near, [a for own, first in project_sets for _, _, a in own + first]
+    )
+    project_held = later_stages(refilled(project_sets, arrays))
+    attend_far, fed_after = feed(
+        chunks[-1:], (0, 0), False, gain_feed, gain_attend, expand_full, shrink_pieces
+    )
+    attend_far, arrays = barrier(attend_far, [a for _, _, a in project_held])
+    project_pieces = crossed([(*t[:2], a) for t, a in zip(project_held, arrays)])
+    context = attention(attend_near, attend_far, project_pieces)
     return tail_of(
         context, fed_before, after_feed, fed_after, tail_weights,
         gain_conv, gain_final, kernel_taps, batch_scale, batch_shift,

time: 252 us -> 208 us (0.83)
  local copies, waits for them, and re-layouts: 42.5 us -> 9.26 us
  waiting for transfers between devices: 65 us -> 53.9 us
    unnamed x92 -> x83, local copies, waits for them, and re-layouts: 24.2 us -> 5.68 us
    ppermute x28, waiting for transfers between devices: 65 us -> 49.9 us  [send(): return lax.ppermute(array, 'dp', partners(lax.axis_size('dp'), bit))]
    all_gather x1 -> x0, local copies, waits for them, and re-layouts: 12.1 us -> none  [body(): tail_weights = lax.all_gather(tail_rows, 'dp', axis=0)]
    pallas_call x2, Pallas kernels: 41.6 us -> 45.7 us  [feed(): pl.pallas_call(functools.partial(feed_kernel, count, [p[:2] for p in shri...]
    ppermute x3, waiting for transfers between devices: 0.01 us -> 4.02 us  [pass_on(): chunks.append(lax.ppermute(chunks[-1], 'seq', ring))]
    pallas_call x2 -> x1, Pallas kernels: 48.1 us -> 44.3 us  [attention(): pl.pallas_call(functools.partial(attend_kernel, [p[:2] for p in pieces],...]
    slice x3 -> x2, local copies, waits for them, and re-layouts: 2.82 us -> 0.1 us  [halved(): return [rows[:half_of(rows.shape[0])], rows[half_of(rows.shape[0]):]]]
  transfers between devices with their start and end apart: 33 -> 33, of which waited for: 9 -> 20; matrix products, arithmetic and copies ran while one was open for 4% -> 3% of each run, Pallas kernels for 36% -> 43%
where the time goes in v1:
time: 208 us
  Pallas kernels  107 us (51%)
  waiting for transfers between devices  53.9 us (26%)
  starting transfers between devices  20.5 us (10%)
  between operations  13.9 us (7%)
  local copies, waits for them, and re-layouts  9.26 us (4%)
  other arithmetic  3.59 us (2%)
    ppermute x28, waiting for transfers between devices, send(): return lax.ppermute(array, 'dp', partners(lax.axis_size('dp'), bit))  49.9 us
    pallas_call x2, Pallas kernels, feed(): pl.pallas_call(functools.partial(feed_kernel, count, [p[:2] for p in shri...  45.7 us
    pallas_call x1, Pallas kernels, attention(): pl.pallas_call(functools.partial(attend_kernel, [p[:2] for p in pieces],...  44.3 us
    pallas_call x1, Pallas kernels, tail_of(): pl.pallas_call(tail_kernel, out_shape=jax.ShapeDtypeStruct((rows, width),...  16.8 us
    ppermute x28, starting transfers between devices, send(): return lax.ppermute(array, 'dp', partners(lax.axis_size('dp'), bit))  15.8 us
    unnamed x83, local copies, waits for them, and re-layouts  5.68 us
    ppermute x3, starting transfers between devices, pass_on(): chunks.append(lax.ppermute(chunks[-1], 'seq', ring))  4.66 us
  transfers between devices with their start and end apart: 33, of which 20 were waited for; matrix products, arithmetic and copies ran while one was open for 3% of the time, Pallas kernels for 43%

profile of v1, /device:TPU:0, one launch (start us, length us, event | category | flops | bytes accessed | tf_op | source)
XLA Modules:
  0.0 208.0 jit_solution(11521271325463851220)
XLA Ops:
  7.9 1.2 fusion.5
  12.9 3.1 %collective-permute-start.4 = (bf16[512,1024]{1,0:T(8,128)(2,1)}, bf16[512,1024]{1,0:T(8,128)(2,1)}, u32[]{:S(2)}, u32[]{:S(2)}) collective-permute-start(bf16[512,1024]{1,0:T(8,128)(2,1)} %bitcast.refs_0_), channel_id=1, source_target_pairs={{0,1},{1,2},{2,3},{3,0},{4,5},{5,6},{6,7},{7,4},{8,9},{9,10},{10,1... | collective-permute-start | bytes 3145736 | tf_op jit(solution)/shard_map/ppermute | solution.py:525
  16.5 1.4 copy.32
  18.2 1.6 collective-permute-start
  19.7 1.5 collective-permute-start.1
  22.3 14.6 %collective-permute-done.refs_7_.refs_5_ = bf16[64,2816]{1,0:T(8,128)(2,1)} collective-permute-done((bf16[64,2816]{1,0:T(8,128)(2,1)S(1)}, bf16[64,2816]{1,0:T(8,128)(2,1)}, u32[]{:S(2)}, u32[]{:S(2)}) %collective-permute-start) | collective-permute-done | bytes 360480 | tf_op jit(solution)/shard_map/ppermute | solution.py:49
  36.9 1.3 collective-permute-done.1.refs_8_.refs_6_
  38.2 5.4 %collective-permute-done.2.refs_12_.refs_10_ = bf16[64,2816]{1,0:T(8,128)(2,1)S(1)} collective-permute-done((bf16[64,2816]{1,0:T(8,128)(2,1)S(1)}, bf16[64,2816]{1,0:T(8,128)(2,1)S(1)}, u32[]{:S(2)}, u32[]{:S(2)}) %collective-permute-start.2) | collective-permute-done | bytes 360480 | tf_op jit(solution)/shard_map/ppermute | solution.py:49
  43.5 1.3 collective-permute-done.3.refs_11_.refs_9_
  44.9 1.6 collective-permute-start.7
  46.9 1.6 collective-permute-start.5
  50.1 15.4 %collective-permute-done.5.refs_9_.refs_7_ = bf16[64,2816]{1,0:T(8,128)(2,1)S(1)} collective-permute-done((bf16[64,2816]{1,0:T(8,128)(2,1)}, bf16[64,2816]{1,0:T(8,128)(2,1)S(1)}, u32[]{:S(2)}, u32[]{:S(2)}) %collective-permute-start.5) | collective-permute-done | bytes 360480 | tf_op jit(solution)/shard_map/ppermute | solution.py:49
  65.5 1.5 collective-permute-done.6.refs_13_.refs_11_
  67.0 4.0 %collective-permute-done.7.refs_2_ = bf16[512,1024]{1,0:T(8,128)(2,1)} collective-permute-done((bf16[512,1024]{1,0:T(8,128)(2,1)}, bf16[512,1024]{1,0:T(8,128)(2,1)}, u32[]{:S(2)}, u32[]{:S(2)}) %collective-permute-start.7) | collective-permute-done | bytes 1048608 | tf_op jit(solution)/shard_map/ppermute | solution.py:525
  75.1 1.7 collective-permute-start.17
  76.9 1.8 collective-permute-start.18
  79.4 31.3 %feed.2 = (bf16[1536,1024]{1,0:T(8,128)(2,1)}, f32[16,1024]{1,0:T(8,128)}, f32[512,1024]{1,0:T(8,128)}) custom-call(bf16[512,1024]{1,0:T(8,128)(2,1)} %bitcast.refs_0_, bf16[512,1024]{1,0:T(8,128)(2,1)} %collective-permute-done.4.refs_1_, bf16[512,1024]{1,0:T(8,128)(2,1)} %collective-permute-done.7.refs_2_, f32[1,1024]{1,0:T(1,128)} %bitcast.74, ...), custom_call_target="tpu_custom_call" | custom-call | flops 17716740096 | bytes 17825792 | tf_op jit(solution)/shard_map/feed/pallas_call | solution.py:214
  110.8 1.8 collective-permute-start.21
  113.6 14.4 %feed.3 = (bf16[512,1024]{1,0:T(8,128)(2,1)}, f32[16,1024]{1,0:T(8,128)}) custom-call(bf16[512,1024]{1,0:T(8,128)(2,1)} %copy-done.14, f32[1,1024]{1,0:T(1,128)} %bitcast.75, f32[1,1024]{1,0:T(1,128)} %bitcast.77, bf16[2816,1024]{1,0:T(8,128)(2,1)} %all-gather.4.cloned.1.call-done.refs_5_.refs_3_, bf16[64,2816]{1,0:T(8,128)(2,1)} %copy-done.6, ...), custom_call_target="tpu_custom_call" | custom-call | flops 5905580032 | bytes 13631488 | tf_op jit(solution)/shard_map/feed/pallas_call | solution.py:214
  128.0 2.7 %collective-permute-done.21.refs_5_ = bf16[192,1024]{1,0:T(8,128)(2,1)S(1)} collective-permute-done((bf16[192,1024]{1,0:T(8,128)(2,1)S(1)}, bf16[192,1024]{1,0:T(8,128)(2,1)S(1)}, u32[]{:S(2)}, u32[]{:S(2)}) %collective-permute-start.21) | collective-permute-done | bytes 393248 | tf_op jit(solution)/shard_map/ppermute | solution.py:49
  130.7 1.6 collective-permute-done.22.refs_9_
  136.6 1.2 collective-permute-done.28.refs_15_
  139.9 44.3 %attention.1.context = bf16[544,1024]{1,0:T(8,128)(2,1)} custom-call(bf16[1536,1024]{1,0:T(8,128)(2,1)} %get-tuple-element.63.refs_0_, bf16[512,1024]{1,0:T(8,128)(2,1)} %get-tuple-element.71.refs_1_, bf16[192,1024]{1,0:T(8,128)(2,1)} %copy-done.4, bf16[192,1024]{1,0:T(8,128)(2,1)} %copy-done.15, bf16[192,1024]{1,0:T(8,128)(2,1)} %copy-done.16, ...), custom_call_target="tpu_custom_call" | custom-call | flops 27984396288 | bytes 13828096 | tf_op jit(solution)/shard_map/attention/pallas_call | solution.py:362
  184.3 16.8 %tail.1 = bf16[512,1024]{1,0:T(8,128)(2,1)} custom-call(bf16[544,1024]{1,0:T(8,128)(2,1)} %attention.1.context, f32[16,1024]{1,0:T(8,128)} %get-tuple-element.80.fed_before, f32[512,1024]{1,0:T(8,128)} %get-tuple-element.81.fed_own, f32[16,1024]{1,0:T(8,128)} %get-tuple-element.82.fed_after, bf16[8,512,1024]{2,1,0:T(8,128)(2,1)} %bitcast.73, ...), custom_call_target="tpu_custom_call" | custom-call | flops 4595908608 | bytes 13631488 | tf_op jit(solution)/shard_map/tail/pallas_call | solution.py:468
  (151 shorter events, 21.0 us)
Async XLA Ops:
  6.5 72.9 %all-gather.4.cloned.1.call-start = ((), (), s32[]{:S(2)}) async-start(), calls=%async_computation | async-start | bytes 6488064 | tf_op jit(solution)/shard_map/all_gather | solution.py:30
  9.2 175.1 %all-gather.6.cloned.1.call-start = ((), (), s32[]{:S(2)}) async-start(), calls=%async_computation.1 | async-start | bytes 9437184 | tf_op jit(solution)/shard_map/all_gather | solution.py:540
  12.9 31.9 %collective-permute-start.4 = (bf16[512,1024]{1,0:T(8,128)(2,1)}, bf16[512,1024]{1,0:T(8,128)(2,1)}, u32[]{:S(2)}, u32[]{:S(2)}) collective-permute-start(bf16[512,1024]{1,0:T(8,128)(2,1)} %bitcast.refs_0_), channel_id=1, source_target_pairs={{0,1},{1,2},{2,3},{3,0},{4,5},{5,6},{6,7},{7,4},{8,9},{9,10},{10,1... | collective-permute-start | bytes 3145736 | tf_op jit(solution)/shard_map/ppermute | solution.py:525
  18.2 18.7 %collective-permute-start = (bf16[64,2816]{1,0:T(8,128)(2,1)S(1)}, bf16[64,2816]{1,0:T(8,128)(2,1)}, u32[]{:S(2)}, u32[]{:S(2)}) collective-permute-start(bf16[64,2816]{1,0:T(8,128)(2,1)S(1)} %get-tuple-element.52.refs_6_.refs_4_), channel_id=1, source_target_pairs={{0,8},{4,12},{8,0},{12,4},{16,24},{20,28},{24,16},{28,20},{1,9},{5... | collective-permute-start | bytes 1081352 | tf_op jit(solution)/shard_map/ppermute | solution.py:49
  19.7 18.5 %collective-permute-start.1 = (bf16[64,2816]{1,0:T(8,128)(2,1)S(1)}, bf16[64,2816]{1,0:T(8,128)(2,1)S(1)}, u32[]{:S(2)}, u32[]{:S(2)}) collective-permute-start(bf16[64,2816]{1,0:T(8,128)(2,1)S(1)} %get-tuple-element.52.refs_6_.refs_4_), channel_id=1, source_target_pairs={{0,16},{4,20},{8,24},{12,28},{16,0},{20,4},{24,8},{28,12},{1,17},{... | collective-permute-start | bytes 1081352 | tf_op jit(solution)/shard_map/ppermute | solution.py:49
  21.2 22.3 %collective-permute-start.2 = (bf16[64,2816]{1,0:T(8,128)(2,1)S(1)}, bf16[64,2816]{1,0:T(8,128)(2,1)S(1)}, u32[]{:S(2)}, u32[]{:S(2)}) collective-permute-start(bf16[64,2816]{1,0:T(8,128)(2,1)S(1)} %get-tuple-element.56.refs_10_.refs_8_), channel_id=1, source_target_pairs={{0,8},{4,12},{8,0},{12,4},{16,24},{20,28},{24,16},{28,20},{1,9},{5... | collective-permute-start | bytes 1081352 | tf_op jit(solution)/shard_map/ppermute | solution.py:49
  21.8 23.1 %collective-permute-start.3 = (bf16[64,2816]{1,0:T(8,128)(2,1)S(1)}, bf16[64,2816]{1,0:T(8,128)(2,1)}, u32[]{:S(2)}, u32[]{:S(2)}) collective-permute-start(bf16[64,2816]{1,0:T(8,128)(2,1)S(1)} %get-tuple-element.56.refs_10_.refs_8_), channel_id=1, source_target_pairs={{0,16},{4,20},{8,24},{12,28},{16,0},{20,4},{24,8},{28,12},{1,17},{... | collective-permute-start | bytes 1081352 | tf_op jit(solution)/shard_map/ppermute | solution.py:49
  44.9 26.1 %collective-permute-start.7 = (bf16[512,1024]{1,0:T(8,128)(2,1)}, bf16[512,1024]{1,0:T(8,128)(2,1)}, u32[]{:S(2)}, u32[]{:S(2)}) collective-permute-start(bf16[512,1024]{1,0:T(8,128)(2,1)} %collective-permute-done.4.refs_1_), channel_id=1, source_target_pairs={{0,1},{1,2},{2,3},{3,0},{4,5},{5,6},{6,7},{7,4},{8,9},{9,10},{10,1... | collective-permute-start | bytes 3145736 | tf_op jit(solution)/shard_map/ppermute | solution.py:525
  46.9 18.6 %collective-permute-start.5 = (bf16[64,2816]{1,0:T(8,128)(2,1)}, bf16[64,2816]{1,0:T(8,128)(2,1)S(1)}, u32[]{:S(2)}, u32[]{:S(2)}) collective-permute-start(bf16[64,2816]{1,0:T(8,128)(2,1)} %collective-permute-done.refs_7_.refs_5_), channel_id=1, source_target_pairs={{0,16},{4,20},{8,24},{12,28},{16,0},{20,4},{24,8},{28,12},{1,17},{... | collective-permute-start | bytes 1081352 | tf_op jit(solution)/shard_map/ppermute | solution.py:49
  48.5 18.5 %collective-permute-start.6 = (bf16[64,2816]{1,0:T(8,128)(2,1)}, bf16[64,2816]{1,0:T(8,128)(2,1)S(1)}, u32[]{:S(2)}, u32[]{:S(2)}) collective-permute-start(bf16[64,2816]{1,0:T(8,128)(2,1)} %collective-permute-done.3.refs_11_.refs_9_), channel_id=1, source_target_pairs={{0,8},{4,12},{8,0},{12,4},{16,24},{20,28},{24,16},{28,20},{1,9},{5... | collective-permute-start | bytes 1081352 | tf_op jit(solution)/shard_map/ppermute | solution.py:49
  72.0 3.1 %collective-permute-start.14 = (bf16[64,2816]{1,0:T(8,128)(2,1)S(1)}, bf16[64,2816]{1,0:T(8,128)(2,1)S(1)}, u32[]{:S(2)}, u32[]{:S(2)}) collective-permute-start(bf16[64,2816]{1,0:T(8,128)(2,1)S(1)} %collective-permute-done.2.refs_12_.refs_10_), channel_id=1, source_target_pairs={{0,4},{4,0},{8,12},{12,8},{16,20},{20,16},{24,28},{28,24},{1,5},{5... | collective-permute-start | bytes 1081352 | tf_op jit(solution)/shard_map/ppermute | solution.py:49
  72.7 4.2 %collective-permute-start.15 = (bf16[64,2816]{1,0:T(8,128)(2,1)S(1)}, bf16[64,2816]{1,0:T(8,128)(2,1)S(1)}, u32[]{:S(2)}, u32[]{:S(2)}) collective-permute-start(bf16[64,2816]{1,0:T(8,128)(2,1)S(1)} %collective-permute-done.6.refs_13_.refs_11_), channel_id=1, source_target_pairs={{0,4},{4,0},{8,12},{12,8},{16,20},{20,16},{24,28},{28,24},{1,5},{5... | collective-permute-start | bytes 1081352 | tf_op jit(solution)/shard_map/ppermute | solution.py:49
  73.2 5.5 %collective-permute-start.8 = (bf16[64,2816]{1,0:T(8,128)(2,1)S(1)}, bf16[64,2816]{1,0:T(8,128)(2,1)S(1)}, u32[]{:S(2)}, u32[]{:S(2)}) collective-permute-start(bf16[64,2816]{1,0:T(8,128)(2,1)S(1)} %get-tuple-element.52.refs_6_.refs_4_), channel_id=1, source_target_pairs={{0,4},{4,0},{8,12},{12,8},{16,20},{20,16},{24,28},{28,24},{1,5},{5... | collective-permute-start | bytes 1081352 | tf_op jit(solution)/shard_map/ppermute | solution.py:49
  74.2 4.5 %collective-permute-start.9 = (bf16[64,2816]{1,0:T(8,128)(2,1)}, bf16[64,2816]{1,0:T(8,128)(2,1)}, u32[]{:S(2)}, u32[]{:S(2)}) collective-permute-start(bf16[64,2816]{1,0:T(8,128)(2,1)} %collective-permute-done.refs_7_.refs_5_), channel_id=1, source_target_pairs={{0,4},{4,0},{8,12},{12,8},{16,20},{20,16},{24,28},{28,24},{1,5},{5... | collective-permute-start | bytes 1081352 | tf_op jit(solution)/shard_map/ppermute | solution.py:49
  74.4 36.3 %collective-permute-start.16 = (bf16[192,1024]{1,0:T(8,128)(2,1)S(1)}, bf16[192,1024]{1,0:T(8,128)(2,1)S(1)}, u32[]{:S(2)}, u32[]{:S(2)}) collective-permute-start(bf16[192,1024]{1,0:T(8,128)(2,1)S(1)} %get-tuple-element.72.refs_2_), channel_id=1, source_target_pairs={{0,8},{4,12},{8,0},{12,4},{16,24},{20,28},{24,16},{28,20},{1,9},{5... | collective-permute-start | bytes 1179656 | tf_op jit(solution)/shard_map/ppermute | solution.py:49
  75.1 35.6 %collective-permute-start.17 = (bf16[192,1024]{1,0:T(8,128)(2,1)S(1)}, bf16[192,1024]{1,0:T(8,128)(2,1)S(1)}, u32[]{:S(2)}, u32[]{:S(2)}) collective-permute-start(bf16[192,1024]{1,0:T(8,128)(2,1)S(1)} %get-tuple-element.72.refs_2_), channel_id=1, source_target_pairs={{0,16},{4,20},{8,24},{12,28},{16,0},{20,4},{24,8},{28,12},{1,17},{... | collective-permute-start | bytes 1179656 | tf_op jit(solution)/shard_map/ppermute | solution.py:49
  76.9 33.9 %collective-permute-start.18 = (bf16[192,1024]{1,0:T(8,128)(2,1)S(1)}, bf16[192,1024]{1,0:T(8,128)(2,1)S(1)}, u32[]{:S(2)}, u32[]{:S(2)}) collective-permute-start(bf16[192,1024]{1,0:T(8,128)(2,1)S(1)} %get-tuple-element.76.refs_6_), channel_id=1, source_target_pairs={{0,8},{4,12},{8,0},{12,4},{16,24},{20,28},{24,16},{28,20},{1,9},{5... | collective-permute-start | bytes 1179656 | tf_op jit(solution)/shard_map/ppermute | solution.py:49
  78.7 32.1 %collective-permute-start.19 = (bf16[192,1024]{1,0:T(8,128)(2,1)S(1)}, bf16[192,1024]{1,0:T(8,128)(2,1)S(1)}, u32[]{:S(2)}, u32[]{:S(2)}) collective-permute-start(bf16[192,1024]{1,0:T(8,128)(2,1)S(1)} %get-tuple-element.76.refs_6_), channel_id=1, source_target_pairs={{0,16},{4,20},{8,24},{12,28},{16,0},{20,4},{24,8},{28,12},{1,17},{... | collective-permute-start | bytes 1179656 | tf_op jit(solution)/shard_map/ppermute | solution.py:49
  79.4 33.3 %collective-permute-start.20 = (bf16[512,1024]{1,0:T(8,128)(2,1)}, bf16[512,1024]{1,0:T(8,128)(2,1)S(1)}, u32[]{:S(2)}, u32[]{:S(2)}) collective-permute-start(bf16[512,1024]{1,0:T(8,128)(2,1)} %collective-permute-done.7.refs_2_), channel_id=1, source_target_pairs={{0,1},{1,2},{2,3},{3,0},{4,5},{5,6},{6,7},{7,4},{8,9},{9,10},{10,1... | collective-permute-start | bytes 3145736 | tf_op jit(solution)/shard_map/ppermute | solution.py:525
  110.8 19.9 %collective-permute-start.21 = (bf16[192,1024]{1,0:T(8,128)(2,1)S(1)}, bf16[192,1024]{1,0:T(8,128)(2,1)S(1)}, u32[]{:S(2)}, u32[]{:S(2)}) collective-permute-start(bf16[192,1024]{1,0:T(8,128)(2,1)S(1)} %collective-permute-done.16.refs_3_), channel_id=1, source_target_pairs={{0,16},{4,20},{8,24},{12,28},{16,0},{20,4},{24,8},{28,12},{1,17},{... | collective-permute-start | bytes 1179656 | tf_op jit(solution)/shard_map/ppermute | solution.py:49
  112.6 19.8 %collective-permute-start.22 = (bf16[192,1024]{1,0:T(8,128)(2,1)S(1)}, bf16[192,1024]{1,0:T(8,128)(2,1)}, u32[]{:S(2)}, u32[]{:S(2)}) collective-permute-start(bf16[192,1024]{1,0:T(8,128)(2,1)S(1)} %collective-permute-done.19.refs_7_), channel_id=1, source_target_pairs={{0,8},{4,12},{8,0},{12,4},{16,24},{20,28},{24,16},{28,20},{1,9},{5... | collective-permute-start | bytes 1179656 | tf_op jit(solution)/shard_map/ppermute | solution.py:49
  133.4 3.3 %collective-permute-start.27 = (bf16[192,1024]{1,0:T(8,128)(2,1)S(1)}, bf16[192,1024]{1,0:T(8,128)(2,1)S(1)}, u32[]{:S(2)}, u32[]{:S(2)}) collective-permute-start(bf16[192,1024]{1,0:T(8,128)(2,1)S(1)} %get-tuple-element.76.refs_6_), channel_id=1, source_target_pairs={{0,4},{4,0},{8,12},{12,8},{16,20},{20,16},{24,28},{28,24},{1,5},{5... | collective-permute-start | bytes 1179656 | tf_op jit(solution)/shard_map/ppermute | solution.py:49
  134.2 3.6 %collective-permute-start.28 = (bf16[192,1024]{1,0:T(8,128)(2,1)S(1)}, bf16[192,1024]{1,0:T(8,128)(2,1)S(1)}, u32[]{:S(2)}, u32[]{:S(2)}) collective-permute-start(bf16[192,1024]{1,0:T(8,128)(2,1)S(1)} %collective-permute-done.19.refs_7_), channel_id=1, source_target_pairs={{0,4},{4,0},{8,12},{12,8},{16,20},{20,16},{24,28},{28,24},{1,5},{5... | collective-permute-start | bytes 1179656 | tf_op jit(solution)/shard_map/ppermute | solution.py:49
  134.8 3.6 %collective-permute-start.29 = (bf16[192,1024]{1,0:T(8,128)(2,1)S(1)}, bf16[192,1024]{1,0:T(8,128)(2,1)S(1)}, u32[]{:S(2)}, u32[]{:S(2)}) collective-permute-start(bf16[192,1024]{1,0:T(8,128)(2,1)S(1)} %collective-permute-done.18.refs_8_), channel_id=1, source_target_pairs={{0,4},{4,0},{8,12},{12,8},{16,20},{20,16},{24,28},{28,24},{1,5},{5... | collective-permute-start | bytes 1179656 | tf_op jit(solution)/shard_map/ppermute | solution.py:49
  (48 other events, 589.2 us)
Sparse Core Ops, SparseCore 0:
  9.3 61.5 all-gather.3
  72.8 72.5 all-gather.5

commit v2 on v1

--- a/solution.py
+++ b/solution.py
@@ -1,5 +1,4 @@
 import functools
-import math
 
 import jax
 import jax.numpy as jnp
@@ -79,6 +78,50 @@
     return result
 
 
+def first_sends(array):
+    return [(0, None, array)] + [(bit, None, send(array, bit)) for bit in far_bits()]
+
+
+def relays(first):
+    bits = far_bits()
+    arrived = {far: array for far, _, array in first}
+    result = []
+    for number, order in ((0, bits), (1, bits[::-1])):
+        half = arrived[0].shape[0] // 2
+        cut = {bit: arrived[bit][number * half : (number + 1) * half] for bit in bits}
+        held = [(order[0], cut[order[0]])]
+        for bit in order[1:]:
+            sent = [(far ^ bit, send(a, bit)) for far, a in held]
+            held += [(bit, cut[bit])] + sent
+            result += [(far, number, a) for far, a in sent]
+    return result
+
+
+def flat(sets):
+    return [a for own, first in sets for _, _, a in own + first]
+
+
+def split_late(held):
+    near = [0, *far_bits()]
+    return [t for t in held if t[0] in near], [t for t in held if t[0] not in near]
+
+
+def by_part(pieces):
+    return [
+        sorted([(far, a) for far, n, a in pieces if n == part], key=lambda t: t[0])
+        for part in (0, 1)
+    ]
+
+
+def replaced(held, arrays):
+    return [(far, number, a) for (far, number, _), a in zip(held, arrays)]
+
+
+def held_back(arrays, held):
+    arrays, others = barrier(arrays, [a for _, _, a in held])
+    return arrays, replaced(held, others)
+
+
 def crossed(held):
     return stage(held, 1)
 
@@ -94,32 +137,32 @@
     return lax.optimization_barrier(trees)
 
 
-def half_of(share):
-    return -(-share // 32) * 16
-
-
-def halved(rows):
-    return [rows[: half_of(rows.shape[0])], rows[half_of(rows.shape[0]) :]]
-
-
-def copies(pieces, refs, target, sems, share):
+def copies(fars, refs, target, sems):
     own = lax.axis_index("dp")
     made = []
-    for (far, number), ref in zip(pieces, refs):
+    for far, ref in zip(fars, refs):
         owner = own ^ far
-        start = pl.multiple_of(owner * share + number * half_of(share), 16)
+        start = pl.multiple_of(owner * ref.shape[0], 16)
         rows = target.at[pl.ds(start, ref.shape[0]), :]
-        made.append(pltpu.make_async_copy(ref, rows, sems.at[owner, number]))
+        made.append(pltpu.make_async_copy(ref, rows, sems.at[owner]))
     return made
 
 
 def wait_rows(target, sems, share, owners):
-    half = half_of(share)
     for owner in owners:
-        for number in range(2):
-            start = owner * share + number * half
-            rows = target.at[start : start + (share - half if number else half), :]
-            pltpu.make_async_copy(rows, rows, sems.at[owner, number]).wait()
+        rows = target.at[owner * share : (owner + 1) * share, :]
+        pltpu.make_async_copy(rows, rows, sems.at[owner]).wait()
+
+
+def half_copies(marks, refs, target, sems, share):
+    own = lax.axis_index("dp")
+    made = []
+    for (far, number), ref in zip(marks, refs):
+        owner = own ^ far
+        start = pl.multiple_of(owner * share + (number or 0) * (share // 2), 16)
+        rows = target.at[pl.ds(start, ref.shape[0]), :]
+        made.append(pltpu.make_async_copy(ref, rows, sems.at[owner]))
+    return made
 
 
 def kernel_norm(values, gain_row):
@@ -135,35 +178,31 @@
     return half + half * jnp.tanh(half)
 
 
-def feed_kernel(chunks, pieces, share, edge, keep, *refs):
+def feed_kernel(chunks, fars, edges, keep, *refs):
     refs = list(refs)
     tokens = [refs.pop(0) for _ in range(chunks)]
-    gain_feed, gain_attend, expand = refs.pop(0), refs.pop(0), refs.pop(0)
-    shrink_refs = [refs.pop(0) for _ in pieces]
-    attend_in, fed_edge = refs.pop(0), refs.pop(0)
+    gain_feed, gain_attend = refs.pop(0), refs.pop(0)
+    expand_refs = [refs.pop(0) for _ in fars]
+    shrink_refs = [refs.pop(0) for _ in fars]
+    attend_in = refs.pop(0)
+    fed_edges = [refs.pop(0) for _ in edges]
     fed = refs.pop(0) if keep else None
-    held, expand_all, shrink_all, feed_in, hidden, total = refs[:6]
-    token_sems, expand_sems, shrink_sems = refs[6:]
+    held, expand_all, shrink_all, feed_in, hidden, total, token_sems, expand_sems, shrink_sems = refs
     step = pl.program_id(0)
     units, width = expand_all.shape
     block = 256
-
     token_copies = [
         pltpu.make_async_copy(t, held.at[i], token_sems.at[i]) for i, t in enumerate(tokens)
     ]
-    expand_copies = [
-        pltpu.make_async_copy(
-            expand.at[pl.ds(n * block, block), :],
-            expand_all.at[pl.ds(n * block, block), :],
-            expand_sems.at[n],
-        )
-        for n in range(units // block)
-    ]
-    shrink_copies = copies(pieces, shrink_refs, shrink_all, shrink_sems, share)
 
     @pl.when(step == 0)
     def _():
-        for copy in token_copies[:1] + expand_copies + shrink_copies + token_copies[1:]:
+        token_copies[0].start()
+        for copy in copies(fars, expand_refs, expand_all, expand_sems):
+            copy.start()
+        for copy in copies(fars, shrink_refs, shrink_all, shrink_sems):
+            copy.start()
+        for copy in token_copies[1:]:
             copy.start()
 
     for i in range(chunks):
@@ -171,12 +210,12 @@
         def _(i=i):
             token_copies[i].wait()
 
-    feed_in[...] = kernel_norm(held[step].astype(jnp.float32), gain_feed[...]).astype(jnp.bfloat16)
+    own = held[step].astype(jnp.float32)
+    feed_in[...] = kernel_norm(own, gain_feed[...]).astype(jnp.bfloat16)
 
     @pl.when(step == 0)
     def _():
-        for copy in expand_copies:
-            copy.wait()
+        wait_rows(expand_all, expand_sems, units // len(fars), range(len(fars)))
 
     for n in range(units // block):
         piece = slice(n * block, (n + 1) * block)
@@ -184,7 +223,7 @@
 
     @pl.when(step == 0)
     def _():
-        wait_rows(shrink_all, shrink_sems, share, range(width // share))
+        wait_rows(shrink_all, shrink_sems, width // len(fars), range(len(fars)))
 
     for n in range(width // block):
         piece = slice(n * block, (n + 1) * block)
@@ -192,38 +231,39 @@
             hidden[...], shrink_all[piece, :]
         )
     attend_in[...] = kernel_norm(total[...], gain_attend[...]).astype(jnp.bfloat16)
-
     if fed is not None:
 
         @pl.when(step == 0)
         def _():
             fed[...] = total[...]
 
-    @pl.when(step == edge[0])
-    def _():
-        fed_edge[...] = total[edge[1] : edge[1] + HALO, :]
-
-
-def feed(chunks, edge, keep, gain_feed, gain_attend, expand_full, shrink_pieces):
+    for (place, start), fed_edge in zip(edges, fed_edges):
+
+        @pl.when(step == place)
+        def _(start=start, fed_edge=fed_edge):
+            fed_edge[...] = total[start : start + HALO, :]
+
+
+def feed(chunks, edges, keep, gain_feed, gain_attend, expand_pieces, shrink_pieces):
     rows, width = chunks[0].shape
-    units = expand_full.shape[0]
-    count = len(chunks)
+    count, devices = len(chunks), len(expand_pieces)
+    units = devices * expand_pieces[0][1].shape[0]
+    fars = [far for far, _ in expand_pieces]
     anywhere = pl.BlockSpec(memory_space=pltpu.HBM)
     row = pl.BlockSpec((1, width), lambda i: (0, 0))
-    share = width // lax.axis_size("dp")
     return pl.pallas_call(
-        functools.partial(feed_kernel, count, [p[:2] for p in shrink_pieces], share, edge, keep),
+        functools.partial(feed_kernel, count, fars, edges, keep),
         grid=(count,),
         out_shape=[
             jax.ShapeDtypeStruct((count * rows, width), jnp.bfloat16),
-            jax.ShapeDtypeStruct((HALO, width), jnp.float32),
         ]
+        + [jax.ShapeDtypeStruct((HALO, width), jnp.float32)] * len(edges)
         + [jax.ShapeDtypeStruct((rows, width), jnp.float32)] * keep,
-        in_specs=[anywhere] * count + [row, row, anywhere] + [anywhere] * len(shrink_pieces),
+        in_specs=[anywhere] * count + [row, row] + [anywhere] * (2 * devices),
         out_specs=[
             pl.BlockSpec((rows, width), lambda i: (i, 0)),
-            pl.BlockSpec((HALO, width), lambda i: (0, 0)),
         ]
+        + [pl.BlockSpec((HALO, width), lambda i: (0, 0))] * len(edges)
         + [pl.BlockSpec((rows, width), lambda i: (0, 0))] * keep,
         scratch_shapes=[
             pltpu.VMEM((count, rows, width), jnp.bfloat16),
@@ -233,8 +273,8 @@
             pltpu.VMEM((rows, units), jnp.bfloat16),
             pltpu.VMEM((rows, width), jnp.float32),
             pltpu.SemaphoreType.DMA((count,)),
-            pltpu.SemaphoreType.DMA((units // 256,)),
-            pltpu.SemaphoreType.DMA((len(shrink_pieces) // 2, 2)),
+            pltpu.SemaphoreType.DMA((devices,)),
+            pltpu.SemaphoreType.DMA((devices,)),
         ],
         compiler_params=pltpu.CompilerParams(vmem_limit_bytes=VMEM),
         cost_estimate=pl.CostEstimate(
@@ -244,38 +284,39 @@
         ),
         name="feed",
     )(
-        *chunks, gain_feed[None], gain_attend[None], expand_full, *[p[2] for p in shrink_pieces]
-    )
-
-
-def attend_kernel(pieces, share, *refs):
+        *chunks, gain_feed[None], gain_attend[None],
+        *[a for _, a in expand_pieces], *[a for _, a in shrink_pieces],
+    )
+
+
+def attend_kernel(marks, share, *refs):
     near, far = refs[:2]
-    weight_refs = refs[2 : 2 + len(pieces)]
+    weight_refs = refs[2 : 2 + len(marks)]
     out_ref, inputs, query_rows, weights, queries, keys, values, sems, row_sems = refs[
-        2 + len(pieces) :
+        2 + len(marks) :
     ]
     step, steps = pl.program_id(0), pl.num_programs(0)
     length, width = inputs.shape
     rows = query_rows.shape[0] - 2 * HALO
     pairs = width // LANES
-    made = copies(pieces, weight_refs, weights, sems, share)
+    made = half_copies(marks, weight_refs, weights, sems, share)
+    soon = sorted({(part * width + pair * LANES) // share for part in range(3) for pair in (0, 1)})
     row_copies = [
         pltpu.make_async_copy(source, target, row_sems.at[index])
         for index, (source, target) in enumerate(
             (
                 (near.at[0:rows, :], query_rows.at[HALO : HALO + rows, :]),
                 (near.at[2 * rows - HALO : 2 * rows, :], query_rows.at[0:HALO, :]),
-                (far.at[0:HALO, :], query_rows.at[HALO + rows :, :]),
-                (near, inputs.at[0 : length - rows, :]),
-                (far, inputs.at[length - rows :, :]),
+                (near.at[2 * rows : 2 * rows + HALO, :], query_rows.at[HALO + rows :, :]),
+                (near, inputs.at[0 : near.shape[0], :]),
+                (far, inputs.at[near.shape[0] :, :]),
             )
         )
     ]
-    soon = sorted({(part * width + pair * LANES) // share for part in range(3) for pair in (0, 1)})
-
     def project_queries(pair, slot):
         picked = weights[pl.ds(pl.multiple_of(pair * LANES, LANES), LANES), :]
-        queries[slot] = product(query_rows[...], picked).astype(jnp.bfloat16)
+        scaled = product(query_rows[...], picked).astype(jnp.bfloat16) * HEAD ** (-0.5)
+        queries[slot] = scaled.astype(jnp.bfloat16)
 
     def project_pair(pair, slot, start, stop):
         first = pl.ds(pl.multiple_of(width + pair * LANES, LANES), LANES)
@@ -305,7 +346,6 @@
     heads = LANES // HEAD
     tile = query_rows.shape[0] // 2
     lane = lax.broadcasted_iota(jnp.int32, (tile, LANES), 1) // HEAD
-    factor = HEAD ** (-0.5) * math.log2(math.e)
     tiles = [(start, head) for start in (0, tile) for head in range(heads)]
     blocks = [slice(start, start + rows) for start in range(0, length, rows)]
 
@@ -315,7 +355,7 @@
 
     def context_of(scores):
         top = functools.reduce(jnp.maximum, [jnp.max(s, axis=1, keepdims=True) for s in scores])
-        raised = [jnp.exp2((s - top) * factor) for s in scores]
+        raised = [jnp.exp(s - top) for s in scores]
         totals = sum(jnp.sum(r, axis=1, keepdims=True) for r in raised)
         mixed = sum(
             jnp.dot(
@@ -353,14 +393,15 @@
         attend(False)
 
 
-def attention(near, far, pieces):
-    rows, width = far.shape
+def attention(rows, near, far, pieces):
+    width = far.shape[1]
     total = rows + 2 * HALO
-    length = near.shape[0] + rows
+    length = near.shape[0] + far.shape[0]
+    anywhere = pl.BlockSpec(memory_space=pltpu.HBM)
+    marks = [piece[:2] for piece in pieces]
     share = 3 * width // lax.axis_size("dp")
-    anywhere = pl.BlockSpec(memory_space=pltpu.HBM)
     return pl.pallas_call(
-        functools.partial(attend_kernel, [p[:2] for p in pieces], share),
+        functools.partial(attend_kernel, marks, share),
         grid=(width // LANES,),
         out_shape=jax.ShapeDtypeStruct((total, width), jnp.bfloat16),
         in_specs=[anywhere] * (2 + len(pieces)),
@@ -372,7 +413,7 @@
             pltpu.VMEM((2, total, LANES), jnp.bfloat16),
             pltpu.VMEM((2, length, LANES), jnp.bfloat16),
             pltpu.VMEM((2, length, LANES), jnp.bfloat16),
-            pltpu.SemaphoreType.DMA((len(pieces) // 2, 2)),
+            pltpu.SemaphoreType.DMA((lax.axis_size("dp"),)),
             pltpu.SemaphoreType.DMA((5,)),
         ],
         compiler_params=pltpu.CompilerParams(vmem_limit_bytes=VMEM),
@@ -382,32 +423,43 @@
             transcendentals=total * length * width // HEAD,
         ),
         name="attention",
-    )(near, far, *[p[2] for p in pieces])
-
-
-def tail_kernel(
-    context, fed_before, fed_own, fed_after, weights,
-    gain_conv, gain_final, taps, scale, shift,
-    out, w_output, w_widen, w_narrow, stream, conv_in, gated, shifted, activated, sems,
-):
+    )(near, far, *[a for _, _, a in pieces])
+
+
+def tail_kernel(marks, *refs):
+    refs = list(refs)
+    context, fed_before, fed_own, fed_after = (refs.pop(0) for _ in range(4))
+    weight_refs = [refs.pop(0) for _ in marks]
+    gain_conv, gain_final, taps, scale, shift = (refs.pop(0) for _ in range(5))
+    out, w_output, w_widen, w_narrow, stream, conv_in, gated, shifted, activated, sems = refs
     rows, width = out.shape
     total = rows + 2 * HALO
     block = 256
     devices, share = w_output.shape[:2]
-    made = [
-        pltpu.make_async_copy(weights.at[:, pl.ds(start, ref.shape[1]), :], ref, sems.at[index])
-        for index, (start, ref) in enumerate(
-            ((0, w_output), (share, w_widen), (3 * share, w_narrow))
-        )
-    ]
-    for copy in made:
-        copy.start()
+    targets = [(w_output, 0), (w_widen, share), (w_narrow, 3 * share)]
+    own = lax.axis_index("dp")
+    for (far, number), ref in zip(marks, weight_refs):
+        low = (number or 0) * 2 * share
+        high = low + ref.shape[0]
+        for index, (target, start) in enumerate(targets):
+            first, last = max(low, start), min(high, start + target.shape[1])
+            if first < last:
+                pltpu.make_async_copy(
+                    ref.at[first - low : last - low, :],
+                    target.at[own ^ far, first - start : last - start],
+                    sems.at[index, own ^ far],
+                ).start()
+
+    def arrived(index):
+        for owner in range(devices):
+            place = targets[index][0].at[owner]
+            pltpu.make_async_copy(place, place, sems.at[index, owner]).wait()
 
     def rows_of(ref, start):
         each = ref.shape[1]
         return ref[start // each : (start + block) // each].reshape(block, width)
 
-    made[0].wait()
+    arrived(0)
     for start in range(0, width, block):
         columns = slice(start, start + block)
         mixed = product(context[...], rows_of(w_output, start))
@@ -416,7 +468,7 @@
         stream[HALO + rows :, columns] = fed_after[:, columns] + mixed[HALO + rows :]
     conv_in[...] = kernel_norm(stream[...], gain_conv[...]).astype(jnp.bfloat16)
 
-    made[1].wait()
+    arrived(1)
     place = lax.broadcasted_iota(jnp.int32, (total, block), 0)
     here, last = lax.axis_index("seq"), lax.axis_size("seq") - 1
     low = jnp.where(here == 0, HALO, 0)
@@ -452,23 +504,26 @@
 
     lax.fori_loop(0, width // LANES, conv, 0)
 
-    made[2].wait()
+    arrived(2)
     for start in range(0, width, block):
         columns = slice(start, start + block)
         stream[HALO : HALO + rows, columns] += product(activated[...], rows_of(w_narrow, start))
     out[...] = kernel_norm(stream[HALO : HALO + rows, :], gain_final[...]).astype(jnp.bfloat16)
 
 
-def tail_of(context, fed_before, fed_own, fed_after, weights, gain_conv, gain_final, taps, scale, shift):
+def tail_of(context, fed_before, fed_own, fed_after, pieces, gain_conv, gain_final, taps, scale, shift):
     rows, width = fed_own.shape
     total = rows + 2 * HALO
-    devices = weights.shape[0]
+    devices = lax.axis_size("dp")
     share = width // devices
+    marks = [piece[:2] for piece in pieces]
     whole = pl.BlockSpec(memory_space=pltpu.VMEM)
     return pl.pallas_call(
-        tail_kernel,
+        functools.partial(tail_kernel, marks),
         out_shape=jax.ShapeDtypeStruct((rows, width), jnp.bfloat16),
-        in_specs=[whole] * 4 + [pl.BlockSpec(memory_space=pltpu.HBM)] + [whole] * 5,
+        in_specs=[whole] * 4
+        + [pl.BlockSpec(memory_space=pl.ANY)] * len(pieces)
+        + [whole] * 5,
         out_specs=whole,
         scratch_shapes=[
             pltpu.VMEM((devices, share, width), jnp.bfloat16),
@@ -479,9 +534,9 @@
             pltpu.VMEM((total, width), jnp.float32),
             pltpu.VMEM((8, total, LANES), jnp.float32),
             pltpu.VMEM((rows, width), jnp.bfloat16),
-            pltpu.SemaphoreType.DMA((3,)),
+            pltpu.SemaphoreType.DMA((3, devices)),
         ],
-        compiler_params=pltpu.CompilerParams(vmem_limit_bytes=VMEM),
+        compiler_params=pltpu.CompilerParams(vmem_limit_bytes=36 << 20),
         cost_estimate=pl.CostEstimate(
             flops=8 * total * width * width + 2 * KERNEL * rows * width,
             bytes_accessed=8 * width * width + 10 * rows * width,
@@ -489,7 +544,7 @@
         ),
         name="tail",
     )(
-        context, fed_before, fed_own, fed_after, weights,
+        context, fed_before, fed_own, fed_after, *[a for _, _, a in pieces],
         gain_conv[None], gain_final[None], taps, scale[None], shift[None],
     )
 
@@ -519,14 +574,15 @@
     count = lax.axis_size("seq")
     rows = tokens.shape[1]
     ring = [(i, (i + 1) % count) for i in range(count)]
-    chunks = [tokens[0]]
-
-    def pass_on():
-        chunks.append(lax.ppermute(chunks[-1], "seq", ring))
-
-    expand_full = gathered(own_rows_of(expand_value, expand_scale))
-    shrink_sets = first_stages(halved(own_rows_of(shrink_value, shrink_scale)))
-    project_parts = halved(own_rows_of(project_value, project_scale))
+    before = lax.ppermute(tokens[0], "seq", ring)
+    after = lax.ppermute(tokens[0], "seq", [(b, a) for a, b in ring])
+    expand_sets, shrink_sets = (
+        [one]
+        for one in first_stages(
+            [own_rows_of(expand_value, expand_scale), own_rows_of(shrink_value, shrink_scale)]
+        )
+    )
+    project_rows = own_rows_of(project_value, project_scale)
     tail_rows = jnp.concatenate(
         [
             own_rows_of(output_value, output_scale),
@@ -535,41 +591,57 @@
         ],
         axis=0,
     )
-    tail_rows = with_layout_constraint(tail_rows, Layout((0, 1)))
-    tail_weights = with_layout_constraint(
-        lax.all_gather(tail_rows, "dp", axis=0), Layout((0, 1, 2))
-    )
-    pass_on()
-
-    arrays, chunks[-1] = barrier([a for own, first in shrink_sets for _, _, a in own + first], chunks[-1])
-    shrink_sets = refilled(shrink_sets, arrays)
-    shrink_held = later_stages(shrink_sets)
-    pass_on()
-
-    arrays, project_parts, chunks[-1] = barrier(
-        [a for _, _, a in shrink_held], project_parts, chunks[-1]
-    )
-    shrink_held = [(*t[:2], a) for t, a in zip(shrink_held, arrays)]
-    shrink_pieces = crossed(shrink_held)
-    project_sets = first_stages(project_parts)
-    while len(chunks) < count:
-        pass_on()
-
-    attend_near, fed_before, after_feed = feed(
-        chunks[:-1], (1, rows - HALO), True, gain_feed, gain_attend, expand_full, shrink_pieces
-    )
-    attend_near, arrays = barrier(
-        attend_near, [a for own, first in project_sets for _, _, a in own + first]
-    )
-    project_held = later_stages(refilled(project_sets, arrays))
-    attend_far, fed_after = feed(
-        chunks[-1:], (0, 0), False, gain_feed, gain_attend, expand_full, shrink_pieces
-    )
-    attend_far, arrays = barrier(attend_far, [a for _, _, a in project_held])
-    project_pieces = crossed([(*t[:2], a) for t, a in zip(project_held, arrays)])
-    context = attention(attend_near, attend_far, project_pieces)
+
+    arrays, project_rows, tail_rows = barrier(flat(expand_sets), project_rows, tail_rows)
+    expand_near, expand_late = split_late(later_stages(refilled(expand_sets, arrays)))
+    expand_near = crossed(expand_near)
+
+    arrays, expand_near = held_back(flat(shrink_sets), expand_near)
+    shrink_near, shrink_late = split_late(later_stages(refilled(shrink_sets, arrays)))
+    shrink_near = crossed(shrink_near)
+
+    late, pieces, project_rows, tail_rows, before, after = barrier(
+        [t[2] for t in expand_late + shrink_late],
+        [t[2] for t in expand_near + shrink_near],
+        project_rows,
+        tail_rows,
+        before,
+        after,
+    )
+    pieces = replaced(expand_near + shrink_near, pieces)
+    pieces += crossed(replaced(expand_late + shrink_late, late))
+    others = [before]
+    while len(others) < count - 2:
+        others.append(lax.ppermute(others[-1], "seq", ring))
+    others = others[1:]
+    project_near = first_sends(project_rows)
+    project_own = crossed(project_near[:1])
+    tail_own = crossed([(0, None, tail_rows)])
+    expand_pieces, shrink_pieces = by_part(pieces)
+
+    attend_near, fed_before, fed_after, after_feed = feed(
+        [tokens[0], before, after], [(1, rows - HALO), (2, 0)], True,
+        gain_feed, gain_attend, expand_pieces, shrink_pieces,
+    )
+    attend_near, arrays, tail_rows = barrier(
+        attend_near, [t[2] for t in project_near], tail_rows
+    )
+    project_near = replaced(project_near, arrays)
+    project_late = relays(project_near)
+    project_near = project_own + crossed(project_near[1:])
+    tail_far = [
+        (far, None, send(tail_rows, far)) for far in range(2, lax.axis_size("dp"), 2)
+    ]
+    (attend_far,) = feed(
+        others, [], False, gain_feed, gain_attend, expand_pieces, shrink_pieces
+    )
+    attend_far, late = barrier(attend_far, [t[2] for t in project_late])
+    project_pieces = project_near + crossed(replaced(project_late, late))
+    context = attention(rows, attend_near, attend_far, project_pieces)
+    context, arrays = barrier(context, [t[2] for t in tail_far])
+    tail_pieces = tail_own + crossed(replaced(tail_far, arrays))
     return tail_of(
-        context, fed_before, after_feed, fed_after, tail_weights,
+        context, fed_before, after_feed, fed_after, tail_pieces,
         gain_conv, gain_final, kernel_taps, batch_scale, batch_shift,
     )[None]
 

time: 208 us -> 190 us (0.913)
  between operations: 13.9 us -> 0.77 us
  waiting for transfers between devices: 53.9 us -> 44.8 us
  starting transfers between devices: 20.5 us -> 25.8 us
  Pallas kernels: 107 us -> 103 us
  local copies, waits for them, and re-layouts: 9.26 us -> 12.5 us
    ppermute x28 -> x30, waiting for transfers between devices: 49.9 us -> 29 us  [send(): return lax.ppermute(array, 'dp', partners(lax.axis_size('dp'), bit))]
    ppermute x3, waiting for transfers between devices: 4.02 us -> 15.8 us  [the longest x1 15.8 us: body(): after = lax.ppermute(tokens[0], 'seq', [(b, a) for a, b in ring])]
    pallas_call x4, Pallas kernels: 107 us -> 103 us  [the longest x2 44.2 us: feed(): pl.pallas_call(functools.partial(feed_kernel, count, fars, edges, keep),...]
    ppermute x28 -> x30, starting transfers between devices: 15.8 us -> 18.7 us  [send(): return lax.ppermute(array, 'dp', partners(lax.axis_size('dp'), bit))]
    ppermute x3, starting transfers between devices: 4.66 us -> 7.11 us  [the longest x1 4.17 us: body(): after = lax.ppermute(tokens[0], 'seq', [(b, a) for a, b in ring])]
    unnamed x83 -> x73, local copies, waits for them, and re-layouts: 5.68 us -> 7.02 us
  transfers between devices with their start and end apart: 33 -> 33, of which waited for: 20 -> 13; matrix products, arithmetic and copies ran while one was open for 3% -> 4% of each run, Pallas kernels for 43% -> 47%
where the time goes in v2:
time: 190 us
  Pallas kernels  103 us (54%)
  waiting for transfers between devices  44.8 us (24%)
  starting transfers between devices  25.8 us (14%)
  local copies, waits for them, and re-layouts  12.5 us (7%)
  other arithmetic  2.63 us (1%)
    pallas_call x2, Pallas kernels, feed(): pl.pallas_call(functools.partial(feed_kernel, count, fars, edges, keep),...  44.2 us
    pallas_call x1, Pallas kernels, attention(): pl.pallas_call(functools.partial(attend_kernel, marks, share), grid=(widt...  44.2 us
    ppermute x30, waiting for transfers between devices, send(): return lax.ppermute(array, 'dp', partners(lax.axis_size('dp'), bit))  29 us
    ppermute x30, starting transfers between devices, send(): return lax.ppermute(array, 'dp', partners(lax.axis_size('dp'), bit))  18.7 us
    ppermute x1, waiting for transfers between devices, body(): after = lax.ppermute(tokens[0], 'seq', [(b, a) for a, b in ring])  15.8 us
    pallas_call x1, Pallas kernels, tail_of(): pl.pallas_call(functools.partial(tail_kernel, marks), out_shape=jax.Shape...  14.9 us
    unnamed x73, local copies, waits for them, and re-layouts  7.02 us
    ppermute x1, starting transfers between devices, body(): after = lax.ppermute(tokens[0], 'seq', [(b, a) for a, b in ring])  4.17 us
  transfers between devices with their start and end apart: 33, of which 13 were waited for; matrix products, arithmetic and copies ran while one was open for 4% of the time, Pallas kernels for 47%

profile of v2, /device:TPU:0, one launch (start us, length us, event | category | flops | bytes accessed | tf_op | source)
XLA Modules:
  0.0 189.9 jit_solution(8160177864274013763)
XLA Ops:
  1.3 1.3 fusion.5.refs_5_.refs_3_
  2.6 2.9 %collective-permute-start = (bf16[352,1024]{1,0:T(8,128)(2,1)}, bf16[352,1024]{1,0:T(8,128)(2,1)}, u32[]{:S(2)}, u32[]{:S(2)}) collective-permute-start(bf16[352,1024]{1,0:T(8,128)(2,1)} %fusion.5.refs_5_.refs_3_), channel_id=1, source_target_pairs={{0,8},{4,12},{8,0},{12,4},{16,24},{20,28},{24,16},{28,20},{1,9},{5... | collective-permute-start | bytes 2162696 | tf_op jit(solution)/shard_map/ppermute | solution.py:48
  5.6 1.5 collective-permute-start.1
  7.6 1.4 copy.41
  9.8 2.0 %collective-permute-start.12 = (bf16[512,1024]{1,0:T(8,128)(2,1)}, bf16[512,1024]{1,0:T(8,128)(2,1)}, u32[]{:S(2)}, u32[]{:S(2)}) collective-permute-start(bf16[512,1024]{1,0:T(8,128)(2,1)} %bitcast.refs_0_), channel_id=1, source_target_pairs={{0,1},{1,2},{2,3},{3,0},{4,5},{5,6},{6,7},{7,4},{8,9},{9,10},{10,1... | collective-permute-start | bytes 3145736 | tf_op jit(solution)/shard_map/ppermute | solution.py:577
  14.4 8.4 %collective-permute-done.refs_7_.refs_5_ = bf16[352,1024]{1,0:T(8,128)(2,1)} collective-permute-done((bf16[352,1024]{1,0:T(8,128)(2,1)}, bf16[352,1024]{1,0:T(8,128)(2,1)}, u32[]{:S(2)}, u32[]{:S(2)}) %collective-permute-start) | collective-permute-done | bytes 720928 | tf_op jit(solution)/shard_map/ppermute | solution.py:48
  22.8 4.2 %collective-permute-start.13 = (bf16[512,1024]{1,0:T(8,128)(2,1)}, bf16[512,1024]{1,0:T(8,128)(2,1)}, u32[]{:S(2)}, u32[]{:S(2)}) collective-permute-start(bf16[512,1024]{1,0:T(8,128)(2,1)} %bitcast.refs_0_), channel_id=1, source_target_pairs={{1,0},{2,1},{3,2},{0,3},{5,4},{6,5},{7,6},{4,7},{9,8},{10,9},{11,1... | collective-permute-start | bytes 3145736 | tf_op jit(solution)/shard_map/ppermute | solution.py:578
  28.6 8.8 %collective-permute-done.3.refs_15_.refs_13_ = bf16[128,2816]{1,0:T(8,128)(2,1)} collective-permute-done((bf16[128,2816]{1,0:T(8,128)(2,1)S(1)}, bf16[128,2816]{1,0:T(8,128)(2,1)}, u32[]{:S(2)}, u32[]{:S(2)}) %collective-permute-start.3) | collective-permute-done | bytes 720928 | tf_op jit(solution)/shard_map/ppermute | solution.py:48
  37.5 1.5 collective-permute-done.4.refs_17_.refs_15_
  38.9 1.6 collective-permute-start.2
  41.5 1.3 collective-permute-start.8
  42.9 15.8 %collective-permute-done.13.refs_2_ = bf16[512,1024]{1,0:T(8,128)(2,1)} collective-permute-done((bf16[512,1024]{1,0:T(8,128)(2,1)}, bf16[512,1024]{1,0:T(8,128)(2,1)}, u32[]{:S(2)}, u32[]{:S(2)}) %collective-permute-start.13) | collective-permute-done | bytes 1048608 | tf_op jit(solution)/shard_map/ppermute | solution.py:578
  58.7 1.3 collective-permute-done.8.refs_19_.refs_17_
  61.4 1.5 collective-permute-start.16
  62.9 1.5 collective-permute-start.17
  66.2 30.8 %feed.2 = (bf16[1536,1024]{1,0:T(8,128)(2,1)}, f32[16,1024]{1,0:T(8,128)}, f32[16,1024]{1,0:T(8,128)}, f32[512,1024]{1,0:T(8,128)}) custom-call(bf16[512,1024]{1,0:T(8,128)(2,1)} %bitcast.refs_0_, bf16[512,1024]{1,0:T(8,128)(2,1)} %collective-permute-done.12.refs_1_, bf16[512,1024]{1,0:T(8,128)(2,1)} %collective-permute-done.13.refs_2_, f32[1,1024]{1,0:T(1,128)} %bitcast.76, ...), custom_call_target="tpu_custom_call" | custom-call | flops 17716740096 | bytes 17825792 | tf_op jit(solution)/shard_map/feed/pallas_call | solution.py:254
  101.5 13.5 %feed.3.refs_1_ = bf16[512,1024]{1,0:T(8,128)(2,1)} custom-call(bf16[512,1024]{1,0:T(8,128)(2,1)} %collective-permute-done.18.refs_0_, f32[1,1024]{1,0:T(1,128)} %bitcast.77, f32[1,1024]{1,0:T(1,128)} %bitcast.79, bf16[352,1024]{1,0:T(8,128)(2,1)} %fusion.5.refs_5_.refs_3_, bf16[352,1024]{1,0:T(8,128)(2,1)} %copy-done.23, ...), custom_call_target="tpu_custom_call" | custom-call | flops 5905580032 | bytes 13631488 | tf_op jit(solution)/shard_map/feed/pallas_call | solution.py:254
  119.4 1.3 collective-permute-start.28
  120.7 44.2 %attention.1.refs_0_ = bf16[544,1024]{1,0:T(8,128)(2,1)} custom-call(bf16[1536,1024]{1,0:T(8,128)(2,1)} %get-tuple-element.85.refs_0_, bf16[512,1024]{1,0:T(8,128)(2,1)} %feed.3.refs_1_, bf16[384,1024]{1,0:T(8,128)(2,1)} %copy-done.10, bf16[384,1024]{1,0:T(8,128)(2,1)} %copy-done.21, bf16[384,1024]{1,0:T(8,128)(2,1)} %collective-permute-done.16.refs_4_, ...), custom_call_target="tpu_custom_call" | custom-call | flops 27984396288 | bytes 13828096 | tf_op jit(solution)/shard_map/attention/pallas_call | solution.py:403
  166.5 3.6 %collective-permute-done.30.refs_9_ = bf16[512,1024]{1,0:T(8,128)(2,1)S(1)} collective-permute-done((bf16[512,1024]{1,0:T(8,128)(2,1)S(1)}, bf16[512,1024]{1,0:T(8,128)(2,1)S(1)}, u32[]{:S(2)}, u32[]{:S(2)}) %collective-permute-start.30) | collective-permute-done | bytes 1048608 | tf_op jit(solution)/shard_map/ppermute | solution.py:48
  170.4 1.5 collective-permute-done.32.refs_11_
  171.9 1.6 copy-done.5
  173.5 1.2 copy-done.6
  174.8 14.9 %tail.1 = bf16[512,1024]{1,0:T(8,128)(2,1)} custom-call(bf16[544,1024]{1,0:T(8,128)(2,1)S(1)} %copy-done.6, f32[16,1024]{1,0:T(8,128)S(1)} %copy-done.7, f32[512,1024]{1,0:T(8,128)S(1)} %copy-done.5, f32[16,1024]{1,0:T(8,128)S(1)} %copy-done.8, bf16[512,1024]{1,0:T(8,128)(2,1)S(1)} %pad_maximum_fusion.refs_4_, ...), custom_call_target="tpu_custom_call" | custom-call | flops 4595908608 | bytes 13631488 | tf_op jit(solution)/shard_map/tail/pallas_call | solution.py:521
  (139 shorter events, 21.4 us)
Async XLA Ops:
  2.6 20.2 %collective-permute-start = (bf16[352,1024]{1,0:T(8,128)(2,1)}, bf16[352,1024]{1,0:T(8,128)(2,1)}, u32[]{:S(2)}, u32[]{:S(2)}) collective-permute-start(bf16[352,1024]{1,0:T(8,128)(2,1)} %fusion.5.refs_5_.refs_3_), channel_id=1, source_target_pairs={{0,8},{4,12},{8,0},{12,4},{16,24},{20,28},{24,16},{28,20},{1,9},{5... | collective-permute-start | bytes 2162696 | tf_op jit(solution)/shard_map/ppermute | solution.py:48
  5.6 23.0 %collective-permute-start.1 = (bf16[352,1024]{1,0:T(8,128)(2,1)}, bf16[352,1024]{1,0:T(8,128)(2,1)}, u32[]{:S(2)}, u32[]{:S(2)}) collective-permute-start(bf16[352,1024]{1,0:T(8,128)(2,1)} %fusion.5.refs_5_.refs_3_), channel_id=1, source_target_pairs={{0,16},{4,20},{8,24},{12,28},{16,0},{20,4},{24,8},{28,12},{1,17},{... | collective-permute-start | bytes 2162696 | tf_op jit(solution)/shard_map/ppermute | solution.py:48
  9.2 28.3 %collective-permute-start.3 = (bf16[128,2816]{1,0:T(8,128)(2,1)S(1)}, bf16[128,2816]{1,0:T(8,128)(2,1)}, u32[]{:S(2)}, u32[]{:S(2)}) collective-permute-start(bf16[128,2816]{1,0:T(8,128)(2,1)S(1)} %fusion.4.refs_13_.refs_11_), channel_id=1, source_target_pairs={{0,8},{4,12},{8,0},{12,4},{16,24},{20,28},{24,16},{28,20},{1,9},{5... | collective-permute-start | bytes 2162696 | tf_op jit(solution)/shard_map/ppermute | solution.py:48
  9.8 29.2 %collective-permute-start.4 = (bf16[128,2816]{1,0:T(8,128)(2,1)S(1)}, bf16[128,2816]{1,0:T(8,128)(2,1)}, u32[]{:S(2)}, u32[]{:S(2)}) collective-permute-start(bf16[128,2816]{1,0:T(8,128)(2,1)S(1)} %fusion.4.refs_13_.refs_11_), channel_id=1, source_target_pairs={{0,16},{4,20},{8,24},{12,28},{16,0},{20,4},{24,8},{28,12},{1,17},{... | collective-permute-start | bytes 2162696 | tf_op jit(solution)/shard_map/ppermute | solution.py:48
  9.8 33.0 %collective-permute-start.12 = (bf16[512,1024]{1,0:T(8,128)(2,1)}, bf16[512,1024]{1,0:T(8,128)(2,1)}, u32[]{:S(2)}, u32[]{:S(2)}) collective-permute-start(bf16[512,1024]{1,0:T(8,128)(2,1)} %bitcast.refs_0_), channel_id=1, source_target_pairs={{0,1},{1,2},{2,3},{3,0},{4,5},{5,6},{6,7},{7,4},{8,9},{9,10},{10,1... | collective-permute-start | bytes 3145736 | tf_op jit(solution)/shard_map/ppermute | solution.py:577
  22.8 35.9 %collective-permute-start.13 = (bf16[512,1024]{1,0:T(8,128)(2,1)}, bf16[512,1024]{1,0:T(8,128)(2,1)}, u32[]{:S(2)}, u32[]{:S(2)}) collective-permute-start(bf16[512,1024]{1,0:T(8,128)(2,1)} %bitcast.refs_0_), channel_id=1, source_target_pairs={{1,0},{2,1},{3,2},{0,3},{5,4},{6,5},{7,6},{4,7},{9,8},{10,9},{11,1... | collective-permute-start | bytes 3145736 | tf_op jit(solution)/shard_map/ppermute | solution.py:578
  28.5 10.4 %collective-permute-start.6 = (bf16[352,1024]{1,0:T(8,128)(2,1)}, bf16[352,1024]{1,0:T(8,128)(2,1)S(1)}, u32[]{:S(2)}, u32[]{:S(2)}) collective-permute-start(bf16[352,1024]{1,0:T(8,128)(2,1)} %collective-permute-done.refs_7_.refs_5_), channel_id=1, source_target_pairs={{0,4},{4,0},{8,12},{12,8},{16,20},{20,16},{24,28},{28,24},{1,5},{5... | collective-permute-start | bytes 2162696 | tf_op jit(solution)/shard_map/ppermute | solution.py:48
  38.9 19.8 %collective-permute-start.2 = (bf16[352,1024]{1,0:T(8,128)(2,1)}, bf16[352,1024]{1,0:T(8,128)(2,1)S(1)}, u32[]{:S(2)}, u32[]{:S(2)}) collective-permute-start(bf16[352,1024]{1,0:T(8,128)(2,1)} %collective-permute-done.refs_7_.refs_5_), channel_id=1, source_target_pairs={{0,16},{4,20},{8,24},{12,28},{16,0},{20,4},{24,8},{28,12},{1,17},{... | collective-permute-start | bytes 2162696 | tf_op jit(solution)/shard_map/ppermute | solution.py:48
  41.3 17.4 %collective-permute-start.10 = (bf16[128,2816]{1,0:T(8,128)(2,1)}, bf16[128,2816]{1,0:T(8,128)(2,1)S(1)}, u32[]{:S(2)}, u32[]{:S(2)}) collective-permute-start(bf16[128,2816]{1,0:T(8,128)(2,1)} %collective-permute-done.4.refs_17_.refs_15_), channel_id=1, source_target_pairs={{0,4},{4,0},{8,12},{12,8},{16,20},{20,16},{24,28},{28,24},{1,5},{5... | collective-permute-start | bytes 2162696 | tf_op jit(solution)/shard_map/ppermute | solution.py:48
  41.5 18.6 %collective-permute-start.8 = (bf16[128,2816]{1,0:T(8,128)(2,1)}, bf16[128,2816]{1,0:T(8,128)(2,1)S(1)}, u32[]{:S(2)}, u32[]{:S(2)}) collective-permute-start(bf16[128,2816]{1,0:T(8,128)(2,1)} %collective-permute-done.4.refs_17_.refs_15_), channel_id=1, source_target_pairs={{0,8},{4,12},{8,0},{12,4},{16,24},{20,28},{24,16},{28,20},{1,9},{5... | collective-permute-start | bytes 2162696 | tf_op jit(solution)/shard_map/ppermute | solution.py:48
  42.8 17.3 %collective-permute-start.11 = (bf16[128,2816]{1,0:T(8,128)(2,1)}, bf16[128,2816]{1,0:T(8,128)(2,1)S(1)}, u32[]{:S(2)}, u32[]{:S(2)}) collective-permute-start(bf16[128,2816]{1,0:T(8,128)(2,1)} %collective-permute-done.3.refs_15_.refs_13_), channel_id=1, source_target_pairs={{0,4},{4,0},{8,12},{12,8},{16,20},{20,16},{24,28},{28,24},{1,5},{5... | collective-permute-start | bytes 2162696 | tf_op jit(solution)/shard_map/ppermute | solution.py:48
  61.4 35.6 %collective-permute-start.16 = (bf16[384,1024]{1,0:T(8,128)(2,1)S(1)}, bf16[384,1024]{1,0:T(8,128)(2,1)}, u32[]{:S(2)}, u32[]{:S(2)}) collective-permute-start(bf16[384,1024]{1,0:T(8,128)(2,1)S(1)} %fusion.3.refs_2_), channel_id=1, source_target_pairs={{0,8},{4,12},{8,0},{12,4},{16,24},{20,28},{24,16},{28,20},{1,9},{5... | collective-permute-start | bytes 2359304 | tf_op jit(solution)/shard_map/ppermute | solution.py:48
  62.9 34.1 %collective-permute-start.17 = (bf16[384,1024]{1,0:T(8,128)(2,1)S(1)}, bf16[384,1024]{1,0:T(8,128)(2,1)}, u32[]{:S(2)}, u32[]{:S(2)}) collective-permute-start(bf16[384,1024]{1,0:T(8,128)(2,1)S(1)} %fusion.3.refs_2_), channel_id=1, source_target_pairs={{0,16},{4,20},{8,24},{12,28},{16,0},{20,4},{24,8},{28,12},{1,17},{... | collective-permute-start | bytes 2359304 | tf_op jit(solution)/shard_map/ppermute | solution.py:48
  64.4 51.2 %collective-permute-start.21 = (bf16[384,1024]{1,0:T(8,128)(2,1)S(1)}, bf16[384,1024]{1,0:T(8,128)(2,1)S(1)}, u32[]{:S(2)}, u32[]{:S(2)}) collective-permute-start(bf16[384,1024]{1,0:T(8,128)(2,1)S(1)} %fusion.3.refs_2_), channel_id=1, source_target_pairs={{0,4},{4,0},{8,12},{12,8},{16,20},{20,16},{24,28},{28,24},{1,5},{5... | collective-permute-start | bytes 2359304 | tf_op jit(solution)/shard_map/ppermute | solution.py:48
  64.5 35.8 %collective-permute-start.18 = (bf16[512,1024]{1,0:T(8,128)(2,1)}, bf16[512,1024]{1,0:T(8,128)(2,1)}, u32[]{:S(2)}, u32[]{:S(2)}) collective-permute-start(bf16[512,1024]{1,0:T(8,128)(2,1)} %collective-permute-done.12.refs_1_), channel_id=1, source_target_pairs={{0,1},{1,2},{2,3},{3,0},{4,5},{5,6},{6,7},{7,4},{8,9},{9,10},{10,1... | collective-permute-start | bytes 3145736 | tf_op jit(solution)/shard_map/ppermute | solution.py:615
  98.1 21.3 %collective-permute-start.22 = (bf16[384,1024]{1,0:T(8,128)(2,1)}, bf16[384,1024]{1,0:T(8,128)(2,1)}, u32[]{:S(2)}, u32[]{:S(2)}) collective-permute-start(bf16[384,1024]{1,0:T(8,128)(2,1)} %collective-permute-done.16.refs_4_), channel_id=1, source_target_pairs={{0,4},{4,0},{8,12},{12,8},{16,20},{20,16},{24,28},{28,24},{1,5},{5... | collective-permute-start | bytes 2359304 | tf_op jit(solution)/shard_map/ppermute | solution.py:48
  99.4 21.3 %collective-permute-start.23 = (bf16[384,1024]{1,0:T(8,128)(2,1)}, bf16[384,1024]{1,0:T(8,128)(2,1)}, u32[]{:S(2)}, u32[]{:S(2)}) collective-permute-start(bf16[384,1024]{1,0:T(8,128)(2,1)} %collective-permute-done.17.refs_5_), channel_id=1, source_target_pairs={{0,4},{4,0},{8,12},{12,8},{16,20},{20,16},{24,28},{28,24},{1,5},{5... | collective-permute-start | bytes 2359304 | tf_op jit(solution)/shard_map/ppermute | solution.py:48
  99.7 15.3 %collective-permute-start.19 = (bf16[192,1024]{1,0:T(8,128)(2,1)S(1)}, bf16[192,1024]{1,0:T(8,128)(2,1)}, u32[]{:S(2)}, u32[]{:S(2)}) collective-permute-start(bf16[192,1024]{1,0:T(8,128)(2,1)S(1)} %slice.6), channel_id=1, source_target_pairs={{0,16},{4,20},{8,24},{12,28},{16,0},{20,4},{24,8},{28,12},{1,17},{... | collective-permute-start | bytes 1179656 | tf_op jit(solution)/shard_map/ppermute | solution.py:48
  100.2 14.8 %collective-permute-start.20 = (bf16[192,1024]{1,0:T(8,128)(2,1)S(1)}, bf16[192,1024]{1,0:T(8,128)(2,1)}, u32[]{:S(2)}, u32[]{:S(2)}) collective-permute-start(bf16[192,1024]{1,0:T(8,128)(2,1)S(1)} %slice.7), channel_id=1, source_target_pairs={{0,8},{4,12},{8,0},{12,4},{16,24},{20,28},{24,16},{28,20},{1,9},{5... | collective-permute-start | bytes 1179656 | tf_op jit(solution)/shard_map/ppermute | solution.py:48
  115.7 50.8 %collective-permute-start.29 = (bf16[512,1024]{1,0:T(8,128)(2,1)S(1)}, bf16[512,1024]{1,0:T(8,128)(2,1)S(1)}, u32[]{:S(2)}, u32[]{:S(2)}) collective-permute-start(bf16[512,1024]{1,0:T(8,128)(2,1)S(1)} %pad_maximum_fusion.refs_4_), channel_id=1, source_target_pairs={{0,4},{4,0},{8,12},{12,8},{16,20},{20,16},{24,28},{28,24},{1,5},{5... | collective-permute-start | bytes 3145736 | tf_op jit(solution)/shard_map/ppermute | solution.py:48
  117.1 47.8 %collective-permute-start.26 = (bf16[512,1024]{1,0:T(8,128)(2,1)S(1)}, bf16[512,1024]{1,0:T(8,128)(2,1)S(1)}, u32[]{:S(2)}, u32[]{:S(2)}) collective-permute-start(bf16[512,1024]{1,0:T(8,128)(2,1)S(1)} %pad_maximum_fusion.refs_4_), channel_id=1, source_target_pairs={{0,8},{4,12},{8,0},{12,4},{16,24},{20,28},{24,16},{28,20},{1,9},{5... | collective-permute-start | bytes 3145736 | tf_op jit(solution)/shard_map/ppermute | solution.py:48
  118.2 47.8 %collective-permute-start.27 = (bf16[512,1024]{1,0:T(8,128)(2,1)S(1)}, bf16[512,1024]{1,0:T(8,128)(2,1)}, u32[]{:S(2)}, u32[]{:S(2)}) collective-permute-start(bf16[512,1024]{1,0:T(8,128)(2,1)S(1)} %pad_maximum_fusion.refs_4_), channel_id=1, source_target_pairs={{0,16},{4,20},{8,24},{12,28},{16,0},{20,4},{24,8},{28,12},{1,17},{... | collective-permute-start | bytes 3145736 | tf_op jit(solution)/shard_map/ppermute | solution.py:48
  119.4 46.6 %collective-permute-start.28 = (bf16[512,1024]{1,0:T(8,128)(2,1)S(1)}, bf16[512,1024]{1,0:T(8,128)(2,1)}, u32[]{:S(2)}, u32[]{:S(2)}) collective-permute-start(bf16[512,1024]{1,0:T(8,128)(2,1)S(1)} %pad_maximum_fusion.refs_4_), channel_id=1, source_target_pairs={{0,24},{4,28},{8,16},{12,20},{16,8},{20,12},{24,0},{28,4},{1,25},{... | collective-permute-start | bytes 3145736 | tf_op jit(solution)/shard_map/ppermute | solution.py:48
  166.5 5.4 %collective-permute-start.32 = (bf16[512,1024]{1,0:T(8,128)(2,1)}, bf16[512,1024]{1,0:T(8,128)(2,1)S(1)}, u32[]{:S(2)}, u32[]{:S(2)}) collective-permute-start(bf16[512,1024]{1,0:T(8,128)(2,1)} %collective-permute-done.28.refs_8_), channel_id=1, source_target_pairs={{0,4},{4,0},{8,12},{12,8},{16,20},{20,16},{24,28},{28,24},{1,5},{5... | collective-permute-start | bytes 3145736 | tf_op jit(solution)/shard_map/ppermute | solution.py:48
  (43 other events, 695.4 us)

commit v3 on v2

--- a/solution.py
+++ b/solution.py
@@ -200,10 +200,6 @@
         token_copies[0].start()
         for copy in copies(fars, expand_refs, expand_all, expand_sems):
             copy.start()
-        for copy in copies(fars, shrink_refs, shrink_all, shrink_sems):
-            copy.start()
-        for copy in token_copies[1:]:
-            copy.start()
 
     for i in range(chunks):
         @pl.when(step == i)
@@ -216,6 +212,8 @@
     @pl.when(step == 0)
     def _():
         wait_rows(expand_all, expand_sems, units // len(fars), range(len(fars)))
+        for copy in copies(fars, shrink_refs, shrink_all, shrink_sems) + token_copies[1:]:
+            copy.start()
 
     for n in range(units // block):
         piece = slice(n * block, (n + 1) * block)
@@ -313,6 +311,18 @@
             )
         )
     ]
+    rest = [owner for owner in range(3 * width // share) if owner not in soon]
+    here = lax.axis_index("dp")
+
+    def start_owned(owners):
+        for (far, _), copy in zip(marks, made):
+            owner = here ^ far
+            wanted = functools.reduce(jnp.logical_or, [owner == o for o in owners])
+
+            @pl.when(wanted)
+            def _(copy=copy):
+                copy.start()
+
     def project_queries(pair, slot):
         picked = weights[pl.ds(pl.multiple_of(pair * LANES, LANES), LANES), :]
         scaled = product(query_rows[...], picked).astype(jnp.bfloat16) * HEAD ** (-0.5)
@@ -328,18 +338,19 @@
 
     @pl.when(step == 0)
     def _():
-        for copy in row_copies + made:
+        for copy in row_copies:
             copy.start()
+        start_owned(soon)
         for copy in row_copies:
             copy.wait()
         wait_rows(weights, sems, share, soon)
+        start_owned(rest)
         project_queries(0, 0)
         for start in range(0, length, rows):
             project_pair(0, 0, start, start + rows)
 
     @pl.when(step == 1)
     def _():
-        rest = [owner for owner in range(3 * width // share) if owner not in soon]
         wait_rows(weights, sems, share, rest)
 
     slot = lax.rem(step, 2)

time: 190 us -> 187 us (0.984)
  Pallas kernels: 103 us -> 99.1 us
    pallas_call x2, Pallas kernels: 44.2 us -> 40.9 us  [feed(): pl.pallas_call(functools.partial(feed_kernel, count, fars, edges, keep),...]
  transfers between devices with their start and end apart: 33 -> 33, of which waited for: 13 -> 13; matrix products, arithmetic and copies ran while one was open for 4% -> 4% of each run, Pallas kernels for 47% -> 45%
where the time goes in v3:
time: 187 us; the launch traced here: 186 us
  Pallas kernels  99.1 us (53%)
  waiting for transfers between devices  45.6 us (24%)
  starting transfers between devices  25.8 us (14%)
  local copies, waits for them, and re-layouts  12.5 us (7%)
  other arithmetic  2.63 us (1%)
    pallas_call x1, Pallas kernels, attention(): pl.pallas_call(functools.partial(attend_kernel, marks, share), grid=(widt...  43.4 us
    pallas_call x2, Pallas kernels, feed(): pl.pallas_call(functools.partial(feed_kernel, count, fars, edges, keep),...  40.9 us
    ppermute x30, waiting for transfers between devices, send(): return lax.ppermute(array, 'dp', partners(lax.axis_size('dp'), bit))  29.8 us
    ppermute x30, starting transfers between devices, send(): return lax.ppermute(array, 'dp', partners(lax.axis_size('dp'), bit))  18.7 us
    ppermute x1, waiting for transfers between devices, body(): after = lax.ppermute(tokens[0], 'seq', [(b, a) for a, b in ring])  15.8 us
    pallas_call x1, Pallas kernels, tail_of(): pl.pallas_call(functools.partial(tail_kernel, marks), out_shape=jax.Shape...  14.9 us
    unnamed x73, local copies, waits for them, and re-layouts  7.02 us
    ppermute x1, starting transfers between devices, body(): after = lax.ppermute(tokens[0], 'seq', [(b, a) for a, b in ring])  4.17 us
  transfers between devices with their start and end apart: 33, of which 13 were waited for; matrix products, arithmetic and copies ran while one was open for 4% of the time, Pallas kernels for 45%

profile of v3, /device:TPU:0, one launch (start us, length us, event | category | flops | bytes accessed | tf_op | source)
XLA Modules:
  0.0 186.5 jit_solution(13259733277580231805)
XLA Ops:
  1.3 1.3 fusion.5.refs_5_.refs_3_
  2.6 2.9 %collective-permute-start = (bf16[352,1024]{1,0:T(8,128)(2,1)}, bf16[352,1024]{1,0:T(8,128)(2,1)}, u32[]{:S(2)}, u32[]{:S(2)}) collective-permute-start(bf16[352,1024]{1,0:T(8,128)(2,1)} %fusion.5.refs_5_.refs_3_), channel_id=1, source_target_pairs={{0,8},{4,12},{8,0},{12,4},{16,24},{20,28},{24,16},{28,20},{1,9},{5... | collective-permute-start | bytes 2162696 | tf_op jit(solution)/shard_map/ppermute | solution.py:48
  5.6 1.5 collective-permute-start.1
  7.6 1.4 copy.41
  9.8 2.0 %collective-permute-start.12 = (bf16[512,1024]{1,0:T(8,128)(2,1)}, bf16[512,1024]{1,0:T(8,128)(2,1)}, u32[]{:S(2)}, u32[]{:S(2)}) collective-permute-start(bf16[512,1024]{1,0:T(8,128)(2,1)} %bitcast.refs_0_), channel_id=1, source_target_pairs={{0,1},{1,2},{2,3},{3,0},{4,5},{5,6},{6,7},{7,4},{8,9},{9,10},{10,1... | collective-permute-start | bytes 3145736 | tf_op jit(solution)/shard_map/ppermute | solution.py:588
  14.4 8.4 %collective-permute-done.refs_7_.refs_5_ = bf16[352,1024]{1,0:T(8,128)(2,1)} collective-permute-done((bf16[352,1024]{1,0:T(8,128)(2,1)}, bf16[352,1024]{1,0:T(8,128)(2,1)}, u32[]{:S(2)}, u32[]{:S(2)}) %collective-permute-start) | collective-permute-done | bytes 720928 | tf_op jit(solution)/shard_map/ppermute | solution.py:48
  22.8 4.2 %collective-permute-start.13 = (bf16[512,1024]{1,0:T(8,128)(2,1)}, bf16[512,1024]{1,0:T(8,128)(2,1)}, u32[]{:S(2)}, u32[]{:S(2)}) collective-permute-start(bf16[512,1024]{1,0:T(8,128)(2,1)} %bitcast.refs_0_), channel_id=1, source_target_pairs={{1,0},{2,1},{3,2},{0,3},{5,4},{6,5},{7,6},{4,7},{9,8},{10,9},{11,1... | collective-permute-start | bytes 3145736 | tf_op jit(solution)/shard_map/ppermute | solution.py:589
  28.6 8.8 %collective-permute-done.3.refs_15_.refs_13_ = bf16[128,2816]{1,0:T(8,128)(2,1)} collective-permute-done((bf16[128,2816]{1,0:T(8,128)(2,1)S(1)}, bf16[128,2816]{1,0:T(8,128)(2,1)}, u32[]{:S(2)}, u32[]{:S(2)}) %collective-permute-start.3) | collective-permute-done | bytes 720928 | tf_op jit(solution)/shard_map/ppermute | solution.py:48
  37.5 1.5 collective-permute-done.4.refs_17_.refs_15_
  38.9 1.6 collective-permute-start.2
  41.5 1.3 collective-permute-start.8
  42.9 15.8 %collective-permute-done.13.refs_2_ = bf16[512,1024]{1,0:T(8,128)(2,1)} collective-permute-done((bf16[512,1024]{1,0:T(8,128)(2,1)}, bf16[512,1024]{1,0:T(8,128)(2,1)}, u32[]{:S(2)}, u32[]{:S(2)}) %collective-permute-start.13) | collective-permute-done | bytes 1048608 | tf_op jit(solution)/shard_map/ppermute | solution.py:589
  58.7 1.3 collective-permute-done.8.refs_19_.refs_17_
  61.4 1.5 collective-permute-start.16
  62.9 1.5 collective-permute-start.17
  66.2 28.8 %feed.2 = (bf16[1536,1024]{1,0:T(8,128)(2,1)}, f32[16,1024]{1,0:T(8,128)}, f32[16,1024]{1,0:T(8,128)}, f32[512,1024]{1,0:T(8,128)}) custom-call(bf16[512,1024]{1,0:T(8,128)(2,1)} %bitcast.refs_0_, bf16[512,1024]{1,0:T(8,128)(2,1)} %collective-permute-done.12.refs_1_, bf16[512,1024]{1,0:T(8,128)(2,1)} %collective-permute-done.13.refs_2_, f32[1,1024]{1,0:T(1,128)} %bitcast.76, ...), custom_call_target="tpu_custom_call" | custom-call | flops 17716740096 | bytes 17825792 | tf_op jit(solution)/shard_map/feed/pallas_call | solution.py:252
  99.5 12.1 %feed.3.refs_1_ = bf16[512,1024]{1,0:T(8,128)(2,1)} custom-call(bf16[512,1024]{1,0:T(8,128)(2,1)} %collective-permute-done.18.refs_0_, f32[1,1024]{1,0:T(1,128)} %bitcast.77, f32[1,1024]{1,0:T(1,128)} %bitcast.79, bf16[352,1024]{1,0:T(8,128)(2,1)} %fusion.5.refs_5_.refs_3_, bf16[352,1024]{1,0:T(8,128)(2,1)} %copy-done.23, ...), custom_call_target="tpu_custom_call" | custom-call | flops 5905580032 | bytes 13631488 | tf_op jit(solution)/shard_map/feed/pallas_call | solution.py:252
  116.0 1.3 collective-permute-start.28
  117.3 43.4 %attention.1.refs_0_ = bf16[544,1024]{1,0:T(8,128)(2,1)} custom-call(bf16[1536,1024]{1,0:T(8,128)(2,1)} %get-tuple-element.85.refs_0_, bf16[512,1024]{1,0:T(8,128)(2,1)} %feed.3.refs_1_, bf16[384,1024]{1,0:T(8,128)(2,1)} %copy-done.10, bf16[384,1024]{1,0:T(8,128)(2,1)} %copy-done.21, bf16[384,1024]{1,0:T(8,128)(2,1)} %collective-permute-done.16.refs_4_, ...), custom_call_target="tpu_custom_call" | custom-call | flops 27984396288 | bytes 13828096 | tf_op jit(solution)/shard_map/attention/pallas_call | solution.py:414
  160.7 1.9 %collective-permute-done.27.refs_7_ = bf16[512,1024]{1,0:T(8,128)(2,1)} collective-permute-done((bf16[512,1024]{1,0:T(8,128)(2,1)S(1)}, bf16[512,1024]{1,0:T(8,128)(2,1)}, u32[]{:S(2)}, u32[]{:S(2)}) %collective-permute-start.27) | collective-permute-done | bytes 1048608 | tf_op jit(solution)/shard_map/ppermute | solution.py:48
  163.1 3.6 %collective-permute-done.30.refs_9_ = bf16[512,1024]{1,0:T(8,128)(2,1)S(1)} collective-permute-done((bf16[512,1024]{1,0:T(8,128)(2,1)S(1)}, bf16[512,1024]{1,0:T(8,128)(2,1)S(1)}, u32[]{:S(2)}, u32[]{:S(2)}) %collective-permute-start.30) | collective-permute-done | bytes 1048608 | tf_op jit(solution)/shard_map/ppermute | solution.py:48
  167.0 1.5 collective-permute-done.32.refs_11_
  168.5 1.6 copy-done.5
  171.4 14.9 %tail.1 = bf16[512,1024]{1,0:T(8,128)(2,1)} custom-call(bf16[544,1024]{1,0:T(8,128)(2,1)S(1)} %copy-done.6, f32[16,1024]{1,0:T(8,128)S(1)} %copy-done.7, f32[512,1024]{1,0:T(8,128)S(1)} %copy-done.5, f32[16,1024]{1,0:T(8,128)S(1)} %copy-done.8, bf16[512,1024]{1,0:T(8,128)(2,1)S(1)} %pad_maximum_fusion.refs_4_, ...), custom_call_target="tpu_custom_call" | custom-call | flops 4595908608 | bytes 13631488 | tf_op jit(solution)/shard_map/tail/pallas_call | solution.py:532
  (139 shorter events, 21.6 us)
Async XLA Ops:
  2.6 20.2 %collective-permute-start = (bf16[352,1024]{1,0:T(8,128)(2,1)}, bf16[352,1024]{1,0:T(8,128)(2,1)}, u32[]{:S(2)}, u32[]{:S(2)}) collective-permute-start(bf16[352,1024]{1,0:T(8,128)(2,1)} %fusion.5.refs_5_.refs_3_), channel_id=1, source_target_pairs={{0,8},{4,12},{8,0},{12,4},{16,24},{20,28},{24,16},{28,20},{1,9},{5... | collective-permute-start | bytes 2162696 | tf_op jit(solution)/shard_map/ppermute | solution.py:48
  5.6 23.0 %collective-permute-start.1 = (bf16[352,1024]{1,0:T(8,128)(2,1)}, bf16[352,1024]{1,0:T(8,128)(2,1)}, u32[]{:S(2)}, u32[]{:S(2)}) collective-permute-start(bf16[352,1024]{1,0:T(8,128)(2,1)} %fusion.5.refs_5_.refs_3_), channel_id=1, source_target_pairs={{0,16},{4,20},{8,24},{12,28},{16,0},{20,4},{24,8},{28,12},{1,17},{... | collective-permute-start | bytes 2162696 | tf_op jit(solution)/shard_map/ppermute | solution.py:48
  9.2 28.3 %collective-permute-start.3 = (bf16[128,2816]{1,0:T(8,128)(2,1)S(1)}, bf16[128,2816]{1,0:T(8,128)(2,1)}, u32[]{:S(2)}, u32[]{:S(2)}) collective-permute-start(bf16[128,2816]{1,0:T(8,128)(2,1)S(1)} %fusion.4.refs_13_.refs_11_), channel_id=1, source_target_pairs={{0,8},{4,12},{8,0},{12,4},{16,24},{20,28},{24,16},{28,20},{1,9},{5... | collective-permute-start | bytes 2162696 | tf_op jit(solution)/shard_map/ppermute | solution.py:48
  9.8 29.2 %collective-permute-start.4 = (bf16[128,2816]{1,0:T(8,128)(2,1)S(1)}, bf16[128,2816]{1,0:T(8,128)(2,1)}, u32[]{:S(2)}, u32[]{:S(2)}) collective-permute-start(bf16[128,2816]{1,0:T(8,128)(2,1)S(1)} %fusion.4.refs_13_.refs_11_), channel_id=1, source_target_pairs={{0,16},{4,20},{8,24},{12,28},{16,0},{20,4},{24,8},{28,12},{1,17},{... | collective-permute-start | bytes 2162696 | tf_op jit(solution)/shard_map/ppermute | solution.py:48
  9.8 33.0 %collective-permute-start.12 = (bf16[512,1024]{1,0:T(8,128)(2,1)}, bf16[512,1024]{1,0:T(8,128)(2,1)}, u32[]{:S(2)}, u32[]{:S(2)}) collective-permute-start(bf16[512,1024]{1,0:T(8,128)(2,1)} %bitcast.refs_0_), channel_id=1, source_target_pairs={{0,1},{1,2},{2,3},{3,0},{4,5},{5,6},{6,7},{7,4},{8,9},{9,10},{10,1... | collective-permute-start | bytes 3145736 | tf_op jit(solution)/shard_map/ppermute | solution.py:588
  22.8 35.9 %collective-permute-start.13 = (bf16[512,1024]{1,0:T(8,128)(2,1)}, bf16[512,1024]{1,0:T(8,128)(2,1)}, u32[]{:S(2)}, u32[]{:S(2)}) collective-permute-start(bf16[512,1024]{1,0:T(8,128)(2,1)} %bitcast.refs_0_), channel_id=1, source_target_pairs={{1,0},{2,1},{3,2},{0,3},{5,4},{6,5},{7,6},{4,7},{9,8},{10,9},{11,1... | collective-permute-start | bytes 3145736 | tf_op jit(solution)/shard_map/ppermute | solution.py:589
  28.5 10.4 %collective-permute-start.6 = (bf16[352,1024]{1,0:T(8,128)(2,1)}, bf16[352,1024]{1,0:T(8,128)(2,1)S(1)}, u32[]{:S(2)}, u32[]{:S(2)}) collective-permute-start(bf16[352,1024]{1,0:T(8,128)(2,1)} %collective-permute-done.refs_7_.refs_5_), channel_id=1, source_target_pairs={{0,4},{4,0},{8,12},{12,8},{16,20},{20,16},{24,28},{28,24},{1,5},{5... | collective-permute-start | bytes 2162696 | tf_op jit(solution)/shard_map/ppermute | solution.py:48
  38.9 19.8 %collective-permute-start.2 = (bf16[352,1024]{1,0:T(8,128)(2,1)}, bf16[352,1024]{1,0:T(8,128)(2,1)S(1)}, u32[]{:S(2)}, u32[]{:S(2)}) collective-permute-start(bf16[352,1024]{1,0:T(8,128)(2,1)} %collective-permute-done.refs_7_.refs_5_), channel_id=1, source_target_pairs={{0,16},{4,20},{8,24},{12,28},{16,0},{20,4},{24,8},{28,12},{1,17},{... | collective-permute-start | bytes 2162696 | tf_op jit(solution)/shard_map/ppermute | solution.py:48
  41.3 17.4 %collective-permute-start.10 = (bf16[128,2816]{1,0:T(8,128)(2,1)}, bf16[128,2816]{1,0:T(8,128)(2,1)S(1)}, u32[]{:S(2)}, u32[]{:S(2)}) collective-permute-start(bf16[128,2816]{1,0:T(8,128)(2,1)} %collective-permute-done.4.refs_17_.refs_15_), channel_id=1, source_target_pairs={{0,4},{4,0},{8,12},{12,8},{16,20},{20,16},{24,28},{28,24},{1,5},{5... | collective-permute-start | bytes 2162696 | tf_op jit(solution)/shard_map/ppermute | solution.py:48
  41.5 18.6 %collective-permute-start.8 = (bf16[128,2816]{1,0:T(8,128)(2,1)}, bf16[128,2816]{1,0:T(8,128)(2,1)S(1)}, u32[]{:S(2)}, u32[]{:S(2)}) collective-permute-start(bf16[128,2816]{1,0:T(8,128)(2,1)} %collective-permute-done.4.refs_17_.refs_15_), channel_id=1, source_target_pairs={{0,8},{4,12},{8,0},{12,4},{16,24},{20,28},{24,16},{28,20},{1,9},{5... | collective-permute-start | bytes 2162696 | tf_op jit(solution)/shard_map/ppermute | solution.py:48
  42.8 17.3 %collective-permute-start.11 = (bf16[128,2816]{1,0:T(8,128)(2,1)}, bf16[128,2816]{1,0:T(8,128)(2,1)S(1)}, u32[]{:S(2)}, u32[]{:S(2)}) collective-permute-start(bf16[128,2816]{1,0:T(8,128)(2,1)} %collective-permute-done.3.refs_15_.refs_13_), channel_id=1, source_target_pairs={{0,4},{4,0},{8,12},{12,8},{16,20},{20,16},{24,28},{28,24},{1,5},{5... | collective-permute-start | bytes 2162696 | tf_op jit(solution)/shard_map/ppermute | solution.py:48
  61.4 33.7 %collective-permute-start.16 = (bf16[384,1024]{1,0:T(8,128)(2,1)S(1)}, bf16[384,1024]{1,0:T(8,128)(2,1)}, u32[]{:S(2)}, u32[]{:S(2)}) collective-permute-start(bf16[384,1024]{1,0:T(8,128)(2,1)S(1)} %fusion.3.refs_2_), channel_id=1, source_target_pairs={{0,8},{4,12},{8,0},{12,4},{16,24},{20,28},{24,16},{28,20},{1,9},{5... | collective-permute-start | bytes 2359304 | tf_op jit(solution)/shard_map/ppermute | solution.py:48
  62.9 32.2 %collective-permute-start.17 = (bf16[384,1024]{1,0:T(8,128)(2,1)S(1)}, bf16[384,1024]{1,0:T(8,128)(2,1)}, u32[]{:S(2)}, u32[]{:S(2)}) collective-permute-start(bf16[384,1024]{1,0:T(8,128)(2,1)S(1)} %fusion.3.refs_2_), channel_id=1, source_target_pairs={{0,16},{4,20},{8,24},{12,28},{16,0},{20,4},{24,8},{28,12},{1,17},{... | collective-permute-start | bytes 2359304 | tf_op jit(solution)/shard_map/ppermute | solution.py:48
  64.4 47.8 %collective-permute-start.21 = (bf16[384,1024]{1,0:T(8,128)(2,1)S(1)}, bf16[384,1024]{1,0:T(8,128)(2,1)S(1)}, u32[]{:S(2)}, u32[]{:S(2)}) collective-permute-start(bf16[384,1024]{1,0:T(8,128)(2,1)S(1)} %fusion.3.refs_2_), channel_id=1, source_target_pairs={{0,4},{4,0},{8,12},{12,8},{16,20},{20,16},{24,28},{28,24},{1,5},{5... | collective-permute-start | bytes 2359304 | tf_op jit(solution)/shard_map/ppermute | solution.py:48
  64.5 33.8 %collective-permute-start.18 = (bf16[512,1024]{1,0:T(8,128)(2,1)}, bf16[512,1024]{1,0:T(8,128)(2,1)}, u32[]{:S(2)}, u32[]{:S(2)}) collective-permute-start(bf16[512,1024]{1,0:T(8,128)(2,1)} %collective-permute-done.12.refs_1_), channel_id=1, source_target_pairs={{0,1},{1,2},{2,3},{3,0},{4,5},{5,6},{6,7},{7,4},{8,9},{9,10},{10,1... | collective-permute-start | bytes 3145736 | tf_op jit(solution)/shard_map/ppermute | solution.py:626
  96.1 19.9 %collective-permute-start.22 = (bf16[384,1024]{1,0:T(8,128)(2,1)}, bf16[384,1024]{1,0:T(8,128)(2,1)}, u32[]{:S(2)}, u32[]{:S(2)}) collective-permute-start(bf16[384,1024]{1,0:T(8,128)(2,1)} %collective-permute-done.16.refs_4_), channel_id=1, source_target_pairs={{0,4},{4,0},{8,12},{12,8},{16,20},{20,16},{24,28},{28,24},{1,5},{5... | collective-permute-start | bytes 2359304 | tf_op jit(solution)/shard_map/ppermute | solution.py:48
  97.4 19.9 %collective-permute-start.23 = (bf16[384,1024]{1,0:T(8,128)(2,1)}, bf16[384,1024]{1,0:T(8,128)(2,1)}, u32[]{:S(2)}, u32[]{:S(2)}) collective-permute-start(bf16[384,1024]{1,0:T(8,128)(2,1)} %collective-permute-done.17.refs_5_), channel_id=1, source_target_pairs={{0,4},{4,0},{8,12},{12,8},{16,20},{20,16},{24,28},{28,24},{1,5},{5... | collective-permute-start | bytes 2359304 | tf_op jit(solution)/shard_map/ppermute | solution.py:48
  97.8 13.9 %collective-permute-start.19 = (bf16[192,1024]{1,0:T(8,128)(2,1)S(1)}, bf16[192,1024]{1,0:T(8,128)(2,1)}, u32[]{:S(2)}, u32[]{:S(2)}) collective-permute-start(bf16[192,1024]{1,0:T(8,128)(2,1)S(1)} %slice.6), channel_id=1, source_target_pairs={{0,16},{4,20},{8,24},{12,28},{16,0},{20,4},{24,8},{28,12},{1,17},{... | collective-permute-start | bytes 1179656 | tf_op jit(solution)/shard_map/ppermute | solution.py:48
  98.3 13.4 %collective-permute-start.20 = (bf16[192,1024]{1,0:T(8,128)(2,1)S(1)}, bf16[192,1024]{1,0:T(8,128)(2,1)}, u32[]{:S(2)}, u32[]{:S(2)}) collective-permute-start(bf16[192,1024]{1,0:T(8,128)(2,1)S(1)} %slice.7), channel_id=1, source_target_pairs={{0,8},{4,12},{8,0},{12,4},{16,24},{20,28},{24,16},{28,20},{1,9},{5... | collective-permute-start | bytes 1179656 | tf_op jit(solution)/shard_map/ppermute | solution.py:48
  112.3 50.8 %collective-permute-start.29 = (bf16[512,1024]{1,0:T(8,128)(2,1)S(1)}, bf16[512,1024]{1,0:T(8,128)(2,1)S(1)}, u32[]{:S(2)}, u32[]{:S(2)}) collective-permute-start(bf16[512,1024]{1,0:T(8,128)(2,1)S(1)} %pad_maximum_fusion.refs_4_), channel_id=1, source_target_pairs={{0,4},{4,0},{8,12},{12,8},{16,20},{20,16},{24,28},{28,24},{1,5},{5... | collective-permute-start | bytes 3145736 | tf_op jit(solution)/shard_map/ppermute | solution.py:48
  113.7 47.0 %collective-permute-start.26 = (bf16[512,1024]{1,0:T(8,128)(2,1)S(1)}, bf16[512,1024]{1,0:T(8,128)(2,1)S(1)}, u32[]{:S(2)}, u32[]{:S(2)}) collective-permute-start(bf16[512,1024]{1,0:T(8,128)(2,1)S(1)} %pad_maximum_fusion.refs_4_), channel_id=1, source_target_pairs={{0,8},{4,12},{8,0},{12,4},{16,24},{20,28},{24,16},{28,20},{1,9},{5... | collective-permute-start | bytes 3145736 | tf_op jit(solution)/shard_map/ppermute | solution.py:48
  114.8 47.8 %collective-permute-start.27 = (bf16[512,1024]{1,0:T(8,128)(2,1)S(1)}, bf16[512,1024]{1,0:T(8,128)(2,1)}, u32[]{:S(2)}, u32[]{:S(2)}) collective-permute-start(bf16[512,1024]{1,0:T(8,128)(2,1)S(1)} %pad_maximum_fusion.refs_4_), channel_id=1, source_target_pairs={{0,16},{4,20},{8,24},{12,28},{16,0},{20,4},{24,8},{28,12},{1,17},{... | collective-permute-start | bytes 3145736 | tf_op jit(solution)/shard_map/ppermute | solution.py:48
  116.0 46.6 %collective-permute-start.28 = (bf16[512,1024]{1,0:T(8,128)(2,1)S(1)}, bf16[512,1024]{1,0:T(8,128)(2,1)}, u32[]{:S(2)}, u32[]{:S(2)}) collective-permute-start(bf16[512,1024]{1,0:T(8,128)(2,1)S(1)} %pad_maximum_fusion.refs_4_), channel_id=1, source_target_pairs={{0,24},{4,28},{8,16},{12,20},{16,8},{20,12},{24,0},{28,4},{1,25},{... | collective-permute-start | bytes 3145736 | tf_op jit(solution)/shard_map/ppermute | solution.py:48
  163.1 5.4 %collective-permute-start.32 = (bf16[512,1024]{1,0:T(8,128)(2,1)}, bf16[512,1024]{1,0:T(8,128)(2,1)S(1)}, u32[]{:S(2)}, u32[]{:S(2)}) collective-permute-start(bf16[512,1024]{1,0:T(8,128)(2,1)} %collective-permute-done.28.refs_8_), channel_id=1, source_target_pairs={{0,4},{4,0},{8,12},{12,8},{16,20},{20,16},{24,28},{28,24},{1,5},{5... | collective-permute-start | bytes 3145736 | tf_op jit(solution)/shard_map/ppermute | solution.py:48
  (43 other events, 693.4 us)
